TPU v7x, 32 devices: a whole 2x2x4 slice. The times are simulated.
32 devices in a mesh: gx: 4 (over y, x), gy: 8 (over z, core).
Axes of the slice: x: 2, y: 2, z: 4, core: 2. Of those that a mesh axis runs over, the one named last changes fastest.
Arguments:
- node_shift: float32 [2, 256, 4096], P(None, 'gx', 'gy'), may hold values from -1.5 to 1.5
- node_speed: float32 [2, 256, 4096], P(None, 'gx', 'gy'), may hold values from -4 to 4
- damage_initial: int32 [2, 256, 4096], P(None, 'gx', 'gy'), may hold values from 0 to 7
- cohesive_markers: int32 [32, 8], P('gx', 'gy'), may hold values from 0 to 1, as said below
- cell_warmth: float32 [128, 2048], P(('gx', 'gy')), may hold values from 0 to 1
- heat_storage: float32 [128, 2048], P(('gx', 'gy')), may hold values from 0.5 to 2
- surface_transfer: float32 [128, 2048], P(('gx', 'gy')), may hold values from 0.1 to 1
- quench_liquid_heat: float32 [128, 2048], P(('gx', 'gy')), may hold values from 0 to 0.3
Outputs:
- displace_new: float32 [2, 256, 4096], P(None, 'gx', 'gy')
- velocity_new: float32 [2, 256, 4096], P(None, 'gx', 'gy')
- damage: bfloat16 [2, 256, 4096], P(None, 'gx', 'gy')
- warmth_after_solve: float32 [128, 2048], P(('gx', 'gy'))
Inputs may be any that keep to these rules, and one draw needn't show every extreme that they name: `cohesive_markers`: within each column, every block of 8 consecutive tile rows starting at a multiple of 8 holds between 1 and 4 ones, and in every draw some block holds exactly 4.
All inputs are finite; a program needn't handle non-finite values.
Results may differ from a plain program's by a relative error of at most 0.001.
Values sent between devices are 32-bit elements; how exact they have to be, the bound alone decides.
A program may use at most 64 MiB of HBM per device.

v0:
```python
import jax
import jax.numpy as jnp
from jax import lax
from jax.sharding import PartitionSpec as P

SR = 8
SEG = 128
SUBSTEPS = 8
ITERS = 4


STIFFNESS = 1.0
EXPANSION = 0.6
SOFTENING_SCALE = 0.25
TIME_STEP = 0.4
DAMPING = 0.05
HEAT_INCREMENT = 1.0
GAP_GAIN = 0.5


def with_halo(value, sides, width):
    for axis, dim in sides:
        count, length = (lax.axis_size(axis), value.shape[dim])
        up = [(i, (i + 1) % count) for i in range(count - 1)]
        down = [(j, i) for i, j in up]
        last = lax.slice_in_dim(value, length - width, length, axis=dim)
        first = lax.slice_in_dim(value, 0, width, axis=dim)
        before = lax.ppermute(last, axis, up)
        after = lax.ppermute(first, axis, down)
        value = jnp.concatenate([before, value, after], axis=dim)
    return value


def softening(opening):
    stretch = jnp.maximum(opening, 0.0)
    return 1.0 - jnp.exp(-stretch * stretch / SOFTENING_SCALE)


def edge_masks(row_first, col_first, height_number_all, width_number, total_rows, total_cols):
    row_index = row_first + jnp.arange(height_number_all, dtype=jnp.int32)
    col_index = col_first + jnp.arange(width_number, dtype=jnp.int32)
    in_rows = (row_index >= 0) & (row_index < total_rows)
    in_cols = (col_index >= 0) & (col_index < total_cols)
    present_horizontal = ((row_index >= 1) & (row_index < total_rows))[:, None] & in_cols[None, :]
    present_vertical = in_rows[:, None] & ((col_index >= 1) & (col_index < total_cols))[None, :]
    return (present_horizontal.astype(jnp.float32), present_vertical.astype(jnp.float32))


def march_forward(state_tensors, dense_mesh_heat, present_horizontal, present_vertical):
    disp_x, disp_y, vel_x, vel_y, dam_x, dam_y, weight = [
        state_tensors[number] for number in range(7)
    ]
    average_horizontal = 0.5 * (dense_mesh_heat[1:, :] + dense_mesh_heat[:-1, :])
    open_x = disp_x[1:, :] - disp_x[:-1, :] - EXPANSION * average_horizontal
    shear_x = disp_y[1:, :] - disp_y[:-1, :]
    new_dx = jnp.maximum(
        dam_x[1:, :], softening(open_x) * weight[1:, :] * present_horizontal[1:, :]
    )
    spring_x = STIFFNESS * (1.0 - new_dx) * present_horizontal[1:, :]
    normal_x = spring_x * open_x
    along_x = spring_x * shear_x
    average_vertical = 0.5 * (dense_mesh_heat[:, 1:] + dense_mesh_heat[:, :-1])
    open_y = disp_y[:, 1:] - disp_y[:, :-1] - EXPANSION * average_vertical
    shear_y = disp_x[:, 1:] - disp_x[:, :-1]
    new_dy = jnp.maximum(dam_y[:, 1:], softening(open_y) * weight[:, 1:] * present_vertical[:, 1:])
    spring_y = STIFFNESS * (1.0 - new_dy) * present_vertical[:, 1:]
    normal_y = spring_y * open_y
    along_y = spring_y * shear_y
    force_x = normal_x[1:, 1:-1] - normal_x[:-1, 1:-1] + (along_y[1:-1, 1:] - along_y[1:-1, :-1])
    force_y = along_x[1:, 1:-1] - along_x[:-1, 1:-1] + (normal_y[1:-1, 1:] - normal_y[1:-1, :-1])
    inner_vx = vel_x[1:-1, 1:-1]
    inner_vy = vel_y[1:-1, 1:-1]
    next_vx = inner_vx + TIME_STEP * (force_x - DAMPING * inner_vx)
    next_vy = inner_vy + TIME_STEP * (force_y - DAMPING * inner_vy)
    next_ux = disp_x[1:-1, 1:-1] + TIME_STEP * next_vx
    next_uy = disp_y[1:-1, 1:-1] + TIME_STEP * next_vy
    return jnp.stack(
        [
            next_ux,
            next_uy,
            next_vx,
            next_vy,
            new_dx[:-1, 1:-1],
            new_dy[1:-1, :-1],
            weight[1:-1, 1:-1],
        ]
    )


def widen_upward(padded):
    middle = padded[1:-1]
    even_rows = 0.75 * middle + 0.25 * padded[:-2]
    odd_rows = 0.75 * middle + 0.25 * padded[2:]
    return jnp.stack([even_rows, odd_rows], axis=1).reshape(2 * middle.shape[0], padded.shape[1])


def widen_sideways(padded):
    middle = padded[:, 1:-1]
    even_cols = 0.75 * middle + 0.25 * padded[:, :-2]
    odd_cols = 0.75 * middle + 0.25 * padded[:, 2:]
    return jnp.stack([even_cols, odd_cols], axis=2).reshape(padded.shape[0], 2 * middle.shape[1])


def kernel_table():
    position = jnp.arange(SEG, dtype=jnp.float32)
    return jnp.exp(-4.0 * jnp.abs(position[:, None] - position[None, :]) / SEG) * (2.0 / SEG)


def radiate(values):
    flattened = values.reshape(-1, SEG)
    product = jnp.dot(
        flattened,
        kernel_table(),
        precision=lax.Precision.HIGHEST,
        preferred_element_type=jnp.float32,
    )
    return product.reshape(values.shape)


def prolonged_warmth(cell_patch_slicer):
    height_number_all, width_number = cell_patch_slicer.shape
    padded = with_halo(cell_patch_slicer[None], (("gx", 1), ("gy", 2)), 3)[0]
    row_index = (
        lax.axis_index("gx") * height_number_all
        - 3
        + jnp.arange(height_number_all + 6, dtype=jnp.int32)
    )
    col_index = (
        lax.axis_index("gy") * width_number - 3 + jnp.arange(width_number + 6, dtype=jnp.int32)
    )
    total_rows = height_number_all * lax.axis_size("gx")
    total_cols = width_number * lax.axis_size("gy")
    padded = jnp.where((row_index == -1)[:, None], jnp.roll(padded, -1, 0), padded)
    padded = jnp.where((row_index == total_rows)[:, None], jnp.roll(padded, 1, 0), padded)
    padded = jnp.where((col_index == -1)[None, :], jnp.roll(padded, -1, 1), padded)
    padded = jnp.where((col_index == total_cols)[None, :], jnp.roll(padded, 1, 1), padded)
    return widen_sideways(widen_upward(padded))


def tile_rim(layered_tensors):
    return with_halo(layered_tensors, (("gx", 1), ("gy", 2)), 1)


def heat_solve(
    cell_warmth,
    heat_storage,
    surface_transfer,
    quench_liquid_heat,
    thermal_impedance,
    margin_wrapper,
    row_first,
    total_rows,
    col_first,
    total_cols,
):
    height_number_all, width_number = cell_warmth.shape
    heat_conductance = (1.0 + 0.5 * cell_warmth) / (1.0 + thermal_impedance)
    layered_tensors = margin_wrapper(jnp.stack([heat_conductance, cell_warmth]))
    padded_cond = layered_tensors[0]
    haloed_warmth = layered_tensors[1]
    row_index = (row_first + jnp.arange(height_number_all, dtype=jnp.int32))[:, None]
    col_index = (col_first + jnp.arange(width_number, dtype=jnp.int32))[None, :]
    cond_down = (
        0.5 * (heat_conductance + padded_cond[:-2, 1:-1]) * (row_index >= 1).astype(jnp.float32)
    )
    cond_up = (
        0.5
        * (heat_conductance + padded_cond[2:, 1:-1])
        * (row_index <= total_rows - 2).astype(jnp.float32)
    )
    cond_left = (
        0.5 * (heat_conductance + padded_cond[1:-1, :-2]) * (col_index >= 1).astype(jnp.float32)
    )
    cond_right = (
        0.5
        * (heat_conductance + padded_cond[1:-1, 2:])
        * (col_index <= total_cols - 2).astype(jnp.float32)
    )
    offsum = cond_down + cond_up + cond_left + cond_right
    diagonal = heat_storage / HEAT_INCREMENT + surface_transfer + offsum
    off_ratio = offsum / diagonal
    bound_low = lax.pmin(jnp.min(1.0 - off_ratio), ("gx", "gy"))
    bound_high = lax.pmax(jnp.max(1.0 + off_ratio), ("gx", "gy"))

    def laplace_action(field, padded):
        return diagonal * field - (
            cond_down * padded[:-2, 1:-1]
            + cond_up * padded[2:, 1:-1]
            + cond_left * padded[1:-1, :-2]
            + cond_right * padded[1:-1, 2:]
        )

    center = 0.5 * (bound_high + bound_low)
    spread = 0.5 * (bound_high - bound_low)
    sigma_ratio = center / spread
    rho_now = 1.0 / sigma_ratio
    forcing_entries = (
        heat_storage / HEAT_INCREMENT * cell_warmth + surface_transfer * quench_liquid_heat
    )
    misfit_norm = forcing_entries - laplace_action(cell_warmth, haloed_warmth)
    direction = misfit_norm / diagonal / center
    answer_state = cell_warmth
    for iteration in range(ITERS):
        answer_state = answer_state + direction
        if iteration + 1 < ITERS:
            padded_dir = margin_wrapper(direction[None])[0]
            misfit_norm = misfit_norm - laplace_action(direction, padded_dir)
            rho_next = 1.0 / (2.0 * sigma_ratio - rho_now)
            direction = rho_next * rho_now * direction + 2.0 * rho_next / spread * (
                misfit_norm / diagonal
            )
            rho_now = rho_next
    return answer_state


def per_device(
    node_shift,
    node_speed,
    damage_initial,
    cohesive_markers,
    cell_warmth,
    heat_storage,
    surface_transfer,
    quench_liquid_heat,
):
    height_number_all, width_number = (node_shift.shape[1], node_shift.shape[2])
    cell_patch_slicer, cap_tile, film_tile, bath_tile = (
        lax.all_to_all(cell_warmth, "gy", split_axis=1, concat_axis=0, tiled=True),
        lax.all_to_all(heat_storage, "gy", split_axis=1, concat_axis=0, tiled=True),
        lax.all_to_all(surface_transfer, "gy", split_axis=1, concat_axis=0, tiled=True),
        lax.all_to_all(quench_liquid_heat, "gy", split_axis=1, concat_axis=0, tiled=True),
    )
    dense_mesh_heat = prolonged_warmth(cell_patch_slicer)
    row_first = lax.axis_index("gx") * height_number_all
    col_first = lax.axis_index("gy") * width_number
    total_rows = height_number_all * lax.axis_size("gx")
    total_cols = width_number * lax.axis_size("gy")
    marking = cohesive_markers[:, 0]
    weight = jnp.broadcast_to(
        jnp.repeat(marking, SR)[:, None], (height_number_all, width_number)
    ).astype(jnp.float32)
    present_horizontal, present_vertical = edge_masks(
        row_first, col_first, height_number_all, width_number, total_rows, total_cols
    )
    start_damage = damage_initial.astype(jnp.float32) * 0.125 * weight[None]
    state_tensors = jnp.stack(
        [
            node_shift[0],
            node_shift[1],
            node_speed[0],
            node_speed[1],
            start_damage[0] * present_horizontal,
            start_damage[1] * present_vertical,
            weight,
        ]
    )
    for round_index in range(SUBSTEPS // 4):
        padded = with_halo(state_tensors, (("gx", 1), ("gy", 2)), 4)
        for inner_step in range(4):
            margin = 4 - inner_step
            mask_x, mask_y = edge_masks(
                row_first - margin,
                col_first - margin,
                height_number_all + 2 * margin,
                width_number + 2 * margin,
                total_rows,
                total_cols,
            )
            warmth_lines = dense_mesh_heat[
                4 - margin : height_number_all + 4 + margin, 4 - margin : width_number + 4 + margin
            ]
            padded = march_forward(padded, warmth_lines, mask_x, mask_y)
        state_tensors = padded
    gap_sum = state_tensors[4] + state_tensors[5]
    glowing = radiate(gap_sum)
    resist_tile = GAP_GAIN * glowing.reshape(height_number_all // 2, 2, width_number // 2, 2).sum(
        axis=(1, 3)
    )
    tile_rows, tile_cols = cell_patch_slicer.shape
    updated_tile = heat_solve(
        cell_patch_slicer,
        cap_tile,
        film_tile,
        bath_tile,
        resist_tile,
        tile_rim,
        lax.axis_index("gx") * tile_rows,
        tile_rows * lax.axis_size("gx"),
        lax.axis_index("gy") * tile_cols,
        tile_cols * lax.axis_size("gy"),
    )
    warmth_after_solve = lax.all_to_all(updated_tile, "gy", split_axis=0, concat_axis=1, tiled=True)
    return (
        state_tensors[0:2],
        state_tensors[2:4],
        state_tensors[4:6].astype(jnp.bfloat16),
        warmth_after_solve,
    )


def solution(mesh):
    return jax.shard_map(
        per_device,
        mesh=mesh,
        in_specs=(
            P(None, "gx", "gy"),
            P(None, "gx", "gy"),
            P(None, "gx", "gy"),
            P("gx", "gy"),
            P(("gx", "gy"), None),
            P(("gx", "gy"), None),
            P(("gx", "gy"), None),
            P(("gx", "gy"), None),
        ),
        out_specs=(
            P(None, "gx", "gy"),
            P(None, "gx", "gy"),
            P(None, "gx", "gy"),
            P(("gx", "gy"), None),
        ),
        check_vma=False,
    )
```

profile of v0, /device:TPU:0, one launch (start us, length us, event | category | flops | bytes accessed | tf_op | source)
XLA Modules:
  0.0 288.8 jit_solution(4326041888483396813)
XLA Ops:
  12.3 5.5 %collective-permute-start = (f32[7,4,512]{2,1,0:T(4,128)S(1)}, f32[7,4,512]{2,1,0:T(4,128)S(1)}, u32[]{:S(2)}, u32[]{:S(2)}) collective-permute-start(f32[7,4,512]{2,1,0:T(4,128)S(1)} %copy.43), channel_id=1, source_target_pairs={{0,8},{8,16},{16,24},{1,9},{9,17},{17,25},{2,10},{10,18},{18,26},{... | collective-permute-start | bytes 172040 | tf_op jit(solution)/shard_map/ppermute | solution.py:28
  17.8 5.4 %all-to-all-start = ((f32[4,8,256]{2,0,1:T(4,128)}), f32[4,8,256]{2,0,1:T(4,128)S(1)}, u32[]{:S(2)}, u32[]{:S(2)}) async-start(f32[4,8,256]{2,0,1:T(4,128)} %bitcast.5), calls=%async_computation | async-start | bytes 65536 | tf_op jit(solution)/shard_map/all_to_all | solution.py:228
  23.5 5.5 %all-to-all-done = f32[4,8,256]{2,0,1:T(4,128)S(1)} async-done(((f32[4,8,256]{2,0,1:T(4,128)}), f32[4,8,256]{2,0,1:T(4,128)S(1)}, u32[]{:S(2)}, u32[]{:S(2)}) %all-to-all-start) | async-done | bytes 32800 | tf_op jit(solution)/shard_map/all_to_all | solution.py:228
  29.0 3.3 %all-to-all-start.1 = ((f32[4,8,256]{2,0,1:T(4,128)}), f32[4,8,256]{2,0,1:T(4,128)S(1)}, u32[]{:S(2)}, u32[]{:S(2)}) async-start(f32[4,8,256]{2,0,1:T(4,128)} %bitcast.45), calls=%async_computation.1 | async-start | bytes 65536 | tf_op jit(solution)/shard_map/all_to_all | solution.py:229
  33.7 4.9 %collective-permute-start.4 = (f32[1,3,256]{2,1,0:T(4,128)S(1)}, f32[1,3,256]{2,1,0:T(4,128)S(1)}, u32[]{:S(2)}, u32[]{:S(2)}) collective-permute-start(f32[1,3,256]{2,1,0:T(4,128)S(1)} %get-tuple-element.140), channel_id=1, source_target_pairs={{0,8},{8,16},{16,24},{1,9},{9,17},{17,25},{2,10},{10,18},{18,26},{... | collective-permute-start | bytes 9224 | tf_op jit(solution)/shard_map/ppermute | solution.py:28
  49.5 4.3 %collective-permute-start.2 = (f32[7,72,4]{1,2,0:T(4,128)S(1)}, f32[7,72,4]{1,2,0:T(4,128)S(1)}, u32[]{:S(2)}, u32[]{:S(2)}) collective-permute-start(f32[7,72,4]{1,2,0:T(4,128)S(1)} %get-tuple-element.98), channel_id=1, source_target_pairs={{0,1},{1,2},{2,3},{3,4},{4,5},{5,6},{6,7},{8,9},{9,10},{10,11},{11... | collective-permute-start | bytes 24200 | tf_op jit(solution)/shard_map/ppermute | solution.py:28
  55.3 3.1 %pad_maximum_fusion = f32[7,72,520]{1,2,0:T(8,128)S(1)} fusion(f32[7,72,4]{1,2,0:T(4,128)S(1)} %collective-permute-done.3, f32[7,4,512]{1,2,0:T(8,128)} %copy.46, f32[7,64,512]{1,2,0:T(8,128)S(1)} %broadcast_dynamic-update-slice_fusion, f32[7,4,512]{1,2,0:T(8,128)} %copy.45, f32[7,72,4]{1,2,0:T(4,128)S(1)} %collective-permute-done.2), kind=kLoop, calls=%fused_computation | loop fusion | flops 1048320 | bytes 2096640 | tf_op jit(solution)/shard_map/concatenate | solution.py:30
  75.0 5.5 %collective-permute-start.8 = (f32[7,4,512]{2,1,0:T(4,128)S(1)}, f32[7,4,512]{2,1,0:T(4,128)S(1)}, u32[]{:S(2)}, u32[]{:S(2)}) collective-permute-start(f32[7,4,512]{2,1,0:T(4,128)S(1)} %copy.51), channel_id=1, source_target_pairs={{0,8},{8,16},{16,24},{1,9},{9,17},{17,25},{2,10},{10,18},{18,26},{... | collective-permute-start | bytes 172040 | tf_op jit(solution)/shard_map/ppermute | solution.py:28
  84.7 6.1 %all-to-all-start.2 = ((f32[4,8,256]{2,0,1:T(4,128)}), f32[4,8,256]{2,0,1:T(4,128)S(1)}, u32[]{:S(2)}, u32[]{:S(2)}) async-start(f32[4,8,256]{2,0,1:T(4,128)} %bitcast.47), calls=%async_computation.2 | async-start | bytes 65536 | tf_op jit(solution)/shard_map/all_to_all | solution.py:230
  96.6 4.9 %all-to-all-start.3 = ((f32[4,8,256]{2,0,1:T(4,128)}), f32[4,8,256]{2,0,1:T(4,128)S(1)}, u32[]{:S(2)}, u32[]{:S(2)}) async-start(f32[4,8,256]{2,0,1:T(4,128)} %bitcast.49), calls=%async_computation.3 | async-start | bytes 65536 | tf_op jit(solution)/shard_map/all_to_all | solution.py:231
  102.2 5.1 %all-to-all-done.3 = f32[4,8,256]{2,0,1:T(4,128)S(1)} async-done(((f32[4,8,256]{2,0,1:T(4,128)}), f32[4,8,256]{2,0,1:T(4,128)S(1)}, u32[]{:S(2)}, u32[]{:S(2)}) %all-to-all-start.3) | async-done | bytes 32800 | tf_op jit(solution)/shard_map/all_to_all | solution.py:231
  119.1 9.8 %reshape_reshape.3 = f32[32,2,256,2]{3,2,1,0:T(8,128)} reshape(f32[256,128]{1,0:T(8,128)S(1)} %fusion.224) | data formatting | bytes 262144 | tf_op jit(solution)/shard_map/reshape;reshape | solution.py:276
  128.9 4.6 %reduce_sum.9 = f32[32,256]{1,0:T(8,128)S(1)} reduce(f32[32,2,256,2]{3,2,1,0:T(8,128)} %reshape_reshape.3, f32[]{:T(128)} %constant.86.clone.1), dimensions={1,3}, to_apply=%region_0.1 | reduce | flops 24576 | bytes 163844 | tf_op jit(solution)/shard_map/reduce_sum | solution.py:276
  134.8 5.5 %collective-permute-start.12 = (f32[2,1,256]{2,1,0:T(1,128)S(1)}, f32[2,1,256]{2,1,0:T(1,128)S(1)}, u32[]{:S(2)}, u32[]{:S(2)}) collective-permute-start(f32[2,1,256]{2,1,0:T(1,128)S(1)} %get-tuple-element.122), channel_id=1, source_target_pairs={{0,8},{8,16},{16,24},{1,9},{9,17},{17,25},{2,10},{10,18},{18,26},{... | collective-permute-start | bytes 6152 | tf_op jit(solution)/shard_map/ppermute | solution.py:28
  142.9 3.3 %collective-permute-start.14 = (f32[2,34,1]{2,1,0:T(8,128)S(1)}, f32[2,34,1]{2,1,0:T(8,128)S(1)}, u32[]{:S(2)}, u32[]{:S(2)}) collective-permute-start(f32[2,34,1]{2,1,0:T(8,128)S(1)} %get-tuple-element.120), channel_id=1, source_target_pairs={{0,1},{1,2},{2,3},{3,4},{4,5},{5,6},{6,7},{8,9},{9,10},{10,11},{11... | collective-permute-start | bytes 824 | tf_op jit(solution)/shard_map/ppermute | solution.py:28
  147.7 44.0 %pmax.7 = f32[]{:T(128)} all-reduce(f32[]{:T(128)} %get-tuple-element.17), channel_id=1, replica_groups=mesh['gx'=4,'gy'=8] {'gx','gy'}, use_global_device_ids=true, to_apply=%region_2.3 | all-reduce | flops 1 | bytes 8 | tf_op jit(solution)/shard_map/pmax | solution.py:183
  191.7 39.4 %pmin.7 = f32[]{:T(128)} all-reduce(f32[]{:T(128)} %get-tuple-element.16), channel_id=1, replica_groups=mesh['gx'=4,'gy'=8] {'gx','gy'}, use_global_device_ids=true, to_apply=%region_4.5 | all-reduce | flops 1 | bytes 8 | tf_op jit(solution)/shard_map/pmin | solution.py:182
  233.9 4.8 %collective-permute-start.16 = (f32[1,1,256]{2,1,0:T(1,128)S(1)}, f32[1,1,256]{2,1,0:T(1,128)S(1)}, u32[]{:S(2)}, u32[]{:S(2)}) collective-permute-start(f32[1,1,256]{2,1,0:T(1,128)S(1)} %get-tuple-element.138), channel_id=1, source_target_pairs={{0,8},{8,16},{16,24},{1,9},{9,17},{17,25},{2,10},{10,18},{18,26},{... | collective-permute-start | bytes 3080 | tf_op jit(solution)/shard_map/ppermute | solution.py:28
  246.9 5.4 %collective-permute-start.20 = (f32[1,1,256]{2,1,0:T(1,128)S(1)}, f32[1,1,256]{2,1,0:T(1,128)S(1)}, u32[]{:S(2)}, u32[]{:S(2)}) collective-permute-start(f32[1,1,256]{2,1,0:T(1,128)S(1)} %get-tuple-element.136), channel_id=1, source_target_pairs={{0,8},{8,16},{16,24},{1,9},{9,17},{17,25},{2,10},{10,18},{18,26},{... | collective-permute-start | bytes 3080 | tf_op jit(solution)/shard_map/ppermute | solution.py:28
  255.1 3.5 %collective-permute-start.22 = (f32[1,34,1]{2,1,0:T(8,128)S(1)}, f32[1,34,1]{2,1,0:T(8,128)S(1)}, u32[]{:S(2)}, u32[]{:S(2)}) collective-permute-start(f32[1,34,1]{2,1,0:T(8,128)S(1)} %get-tuple-element.128), channel_id=1, source_target_pairs={{0,1},{1,2},{2,3},{3,4},{4,5},{5,6},{6,7},{8,9},{9,10},{10,11},{11... | collective-permute-start | bytes 416 | tf_op jit(solution)/shard_map/ppermute | solution.py:28
  260.9 5.5 %collective-permute-start.24 = (f32[1,1,256]{2,1,0:T(1,128)S(1)}, f32[1,1,256]{2,1,0:T(1,128)S(1)}, u32[]{:S(2)}, u32[]{:S(2)}) collective-permute-start(f32[1,1,256]{2,1,0:T(1,128)S(1)} %get-tuple-element.134), channel_id=1, source_target_pairs={{0,8},{8,16},{16,24},{1,9},{9,17},{17,25},{2,10},{10,18},{18,26},{... | collective-permute-start | bytes 3080 | tf_op jit(solution)/shard_map/ppermute | solution.py:28
  269.1 4.9 %collective-permute-start.26 = (f32[1,34,1]{2,1,0:T(8,128)S(1)}, f32[1,34,1]{2,1,0:T(8,128)S(1)}, u32[]{:S(2)}, u32[]{:S(2)}) collective-permute-start(f32[1,34,1]{2,1,0:T(8,128)S(1)} %get-tuple-element.126), channel_id=1, source_target_pairs={{0,1},{1,2},{2,3},{3,4},{4,5},{5,6},{6,7},{8,9},{9,10},{10,11},{11... | collective-permute-start | bytes 416 | tf_op jit(solution)/shard_map/ppermute | solution.py:28
  275.7 6.8 %all-to-all-start.4 = ((f32[8,4,256]{2,1,0:T(4,128)}), f32[8,4,256]{2,1,0:T(4,128)S(1)}, u32[]{:S(2)}, u32[]{:S(2)}) async-start(f32[8,4,256]{2,1,0:T(4,128)} %all_to_all.86), calls=%async_computation.4 | async-start | bytes 65536 | tf_op jit(solution)/shard_map/all_to_all | solution.py:292
  285.1 3.1 %all-to-all-done.4 = f32[8,4,256]{2,1,0:T(4,128)S(1)} async-done(((f32[8,4,256]{2,1,0:T(4,128)}), f32[8,4,256]{2,1,0:T(4,128)S(1)}, u32[]{:S(2)}, u32[]{:S(2)}) %all-to-all-start.4) | async-done | bytes 32800 | tf_op jit(solution)/shard_map/all_to_all | solution.py:292
  (235 shorter events, 89.7 us)
Async XLA Ops:
  9.0 30.2 %collective-permute-start.1 = (f32[7,4,512]{2,1,0:T(4,128)S(1)}, f32[7,4,512]{2,1,0:T(4,128)S(1)}, u32[]{:S(2)}, u32[]{:S(2)}) collective-permute-start(f32[7,4,512]{2,1,0:T(4,128)S(1)} %copy.44), channel_id=1, source_target_pairs={{8,0},{16,8},{24,16},{9,1},{17,9},{25,17},{10,2},{18,10},{26,18},{... | collective-permute-start | bytes 172040 | tf_op jit(solution)/shard_map/ppermute | solution.py:29
  12.3 28.7 %collective-permute-start = (f32[7,4,512]{2,1,0:T(4,128)S(1)}, f32[7,4,512]{2,1,0:T(4,128)S(1)}, u32[]{:S(2)}, u32[]{:S(2)}) collective-permute-start(f32[7,4,512]{2,1,0:T(4,128)S(1)} %copy.43), channel_id=1, source_target_pairs={{0,8},{8,16},{16,24},{1,9},{9,17},{17,25},{2,10},{10,18},{18,26},{... | collective-permute-start | bytes 172040 | tf_op jit(solution)/shard_map/ppermute | solution.py:28
  17.8 11.2 %all-to-all-start = ((f32[4,8,256]{2,0,1:T(4,128)}), f32[4,8,256]{2,0,1:T(4,128)S(1)}, u32[]{:S(2)}, u32[]{:S(2)}) async-start(f32[4,8,256]{2,0,1:T(4,128)} %bitcast.5), calls=%async_computation | async-start | bytes 65536 | tf_op jit(solution)/shard_map/all_to_all | solution.py:228
  29.0 55.7 %all-to-all-start.1 = ((f32[4,8,256]{2,0,1:T(4,128)}), f32[4,8,256]{2,0,1:T(4,128)S(1)}, u32[]{:S(2)}, u32[]{:S(2)}) async-start(f32[4,8,256]{2,0,1:T(4,128)} %bitcast.45), calls=%async_computation.1 | async-start | bytes 65536 | tf_op jit(solution)/shard_map/all_to_all | solution.py:229
  32.4 10.5 %collective-permute-start.5 = (f32[1,3,256]{2,1,0:T(4,128)S(1)}, f32[1,3,256]{2,1,0:T(4,128)S(1)}, u32[]{:S(2)}, u32[]{:S(2)}) collective-permute-start(f32[1,3,256]{2,1,0:T(4,128)S(1)} %get-tuple-element.141), channel_id=1, source_target_pairs={{8,0},{16,8},{24,16},{9,1},{17,9},{25,17},{10,2},{18,10},{26,18},{... | collective-permute-start | bytes 9224 | tf_op jit(solution)/shard_map/ppermute | solution.py:29
  33.7 9.2 %collective-permute-start.4 = (f32[1,3,256]{2,1,0:T(4,128)S(1)}, f32[1,3,256]{2,1,0:T(4,128)S(1)}, u32[]{:S(2)}, u32[]{:S(2)}) collective-permute-start(f32[1,3,256]{2,1,0:T(4,128)S(1)} %get-tuple-element.140), channel_id=1, source_target_pairs={{0,8},{8,16},{16,24},{1,9},{9,17},{17,25},{2,10},{10,18},{18,26},{... | collective-permute-start | bytes 9224 | tf_op jit(solution)/shard_map/ppermute | solution.py:28
  43.0 10.8 %collective-permute-start.7 = (f32[1,38,3]{2,1,0:T(8,128)S(1)}, f32[1,38,3]{2,1,0:T(8,128)S(1)}, u32[]{:S(2)}, u32[]{:S(2)}) collective-permute-start(f32[1,38,3]{2,1,0:T(8,128)S(1)} %get-tuple-element.133), channel_id=1, source_target_pairs={{1,0},{2,1},{3,2},{4,3},{5,4},{6,5},{7,6},{9,8},{10,9},{11,10},{12... | collective-permute-start | bytes 1376 | tf_op jit(solution)/shard_map/ppermute | solution.py:29
  44.3 9.5 %collective-permute-start.6 = (f32[1,38,3]{2,1,0:T(8,128)S(1)}, f32[1,38,3]{2,1,0:T(8,128)S(1)}, u32[]{:S(2)}, u32[]{:S(2)}) collective-permute-start(f32[1,38,3]{2,1,0:T(8,128)S(1)} %get-tuple-element.132), channel_id=1, source_target_pairs={{0,1},{1,2},{2,3},{3,4},{4,5},{5,6},{6,7},{8,9},{9,10},{10,11},{11... | collective-permute-start | bytes 1376 | tf_op jit(solution)/shard_map/ppermute | solution.py:28
  48.2 7.1 %collective-permute-start.3 = (f32[7,72,4]{1,2,0:T(4,128)S(1)}, f32[7,72,4]{1,2,0:T(4,128)S(1)}, u32[]{:S(2)}, u32[]{:S(2)}) collective-permute-start(f32[7,72,4]{1,2,0:T(4,128)S(1)} %get-tuple-element.99), channel_id=1, source_target_pairs={{1,0},{2,1},{3,2},{4,3},{5,4},{6,5},{7,6},{9,8},{10,9},{11,10},{12... | collective-permute-start | bytes 24200 | tf_op jit(solution)/shard_map/ppermute | solution.py:29
  71.7 9.4 %collective-permute-start.9 = (f32[7,4,512]{2,1,0:T(4,128)S(1)}, f32[7,4,512]{2,1,0:T(4,128)S(1)}, u32[]{:S(2)}, u32[]{:S(2)}) collective-permute-start(f32[7,4,512]{2,1,0:T(4,128)S(1)} %copy.52), channel_id=1, source_target_pairs={{8,0},{16,8},{24,16},{9,1},{17,9},{25,17},{10,2},{18,10},{26,18},{... | collective-permute-start | bytes 172040 | tf_op jit(solution)/shard_map/ppermute | solution.py:29
  75.0 7.9 %collective-permute-start.8 = (f32[7,4,512]{2,1,0:T(4,128)S(1)}, f32[7,4,512]{2,1,0:T(4,128)S(1)}, u32[]{:S(2)}, u32[]{:S(2)}) collective-permute-start(f32[7,4,512]{2,1,0:T(4,128)S(1)} %copy.51), channel_id=1, source_target_pairs={{0,8},{8,16},{16,24},{1,9},{9,17},{17,25},{2,10},{10,18},{18,26},{... | collective-permute-start | bytes 172040 | tf_op jit(solution)/shard_map/ppermute | solution.py:28
  84.7 11.9 %all-to-all-start.2 = ((f32[4,8,256]{2,0,1:T(4,128)}), f32[4,8,256]{2,0,1:T(4,128)S(1)}, u32[]{:S(2)}, u32[]{:S(2)}) async-start(f32[4,8,256]{2,0,1:T(4,128)} %bitcast.47), calls=%async_computation.2 | async-start | bytes 65536 | tf_op jit(solution)/shard_map/all_to_all | solution.py:230
  91.8 16.1 %collective-permute-start.11 = (f32[7,72,4]{1,2,0:T(4,128)S(1)}, f32[7,72,4]{1,2,0:T(4,128)S(1)}, u32[]{:S(2)}, u32[]{:S(2)}) collective-permute-start(f32[7,72,4]{1,2,0:T(4,128)S(1)} %get-tuple-element.97), channel_id=1, source_target_pairs={{1,0},{2,1},{3,2},{4,3},{5,4},{6,5},{7,6},{9,8},{10,9},{11,10},{12... | collective-permute-start | bytes 24200 | tf_op jit(solution)/shard_map/ppermute | solution.py:29
  93.1 14.8 %collective-permute-start.10 = (f32[7,72,4]{1,2,0:T(4,128)S(1)}, f32[7,72,4]{1,2,0:T(4,128)S(1)}, u32[]{:S(2)}, u32[]{:S(2)}) collective-permute-start(f32[7,72,4]{1,2,0:T(4,128)S(1)} %get-tuple-element.96), channel_id=1, source_target_pairs={{0,1},{1,2},{2,3},{3,4},{4,5},{5,6},{6,7},{8,9},{9,10},{10,11},{11... | collective-permute-start | bytes 24200 | tf_op jit(solution)/shard_map/ppermute | solution.py:28
  96.6 10.6 %all-to-all-start.3 = ((f32[4,8,256]{2,0,1:T(4,128)}), f32[4,8,256]{2,0,1:T(4,128)S(1)}, u32[]{:S(2)}, u32[]{:S(2)}) async-start(f32[4,8,256]{2,0,1:T(4,128)} %bitcast.49), calls=%async_computation.3 | async-start | bytes 65536 | tf_op jit(solution)/shard_map/all_to_all | solution.py:231
  133.5 7.6 %collective-permute-start.13 = (f32[2,1,256]{2,1,0:T(1,128)S(1)}, f32[2,1,256]{2,1,0:T(1,128)S(1)}, u32[]{:S(2)}, u32[]{:S(2)}) collective-permute-start(f32[2,1,256]{2,1,0:T(1,128)S(1)} %get-tuple-element.123), channel_id=1, source_target_pairs={{8,0},{16,8},{24,16},{9,1},{17,9},{25,17},{10,2},{18,10},{26,18},{... | collective-permute-start | bytes 6152 | tf_op jit(solution)/shard_map/ppermute | solution.py:29
  134.8 6.8 %collective-permute-start.12 = (f32[2,1,256]{2,1,0:T(1,128)S(1)}, f32[2,1,256]{2,1,0:T(1,128)S(1)}, u32[]{:S(2)}, u32[]{:S(2)}) collective-permute-start(f32[2,1,256]{2,1,0:T(1,128)S(1)} %get-tuple-element.122), channel_id=1, source_target_pairs={{0,8},{8,16},{16,24},{1,9},{9,17},{17,25},{2,10},{10,18},{18,26},{... | collective-permute-start | bytes 6152 | tf_op jit(solution)/shard_map/ppermute | solution.py:28
  232.6 7.6 %collective-permute-start.17 = (f32[1,1,256]{2,1,0:T(1,128)S(1)}, f32[1,1,256]{2,1,0:T(1,128)S(1)}, u32[]{:S(2)}, u32[]{:S(2)}) collective-permute-start(f32[1,1,256]{2,1,0:T(1,128)S(1)} %get-tuple-element.139), channel_id=1, source_target_pairs={{8,0},{16,8},{24,16},{9,1},{17,9},{25,17},{10,2},{18,10},{26,18},{... | collective-permute-start | bytes 3080 | tf_op jit(solution)/shard_map/ppermute | solution.py:29
  233.9 6.3 %collective-permute-start.16 = (f32[1,1,256]{2,1,0:T(1,128)S(1)}, f32[1,1,256]{2,1,0:T(1,128)S(1)}, u32[]{:S(2)}, u32[]{:S(2)}) collective-permute-start(f32[1,1,256]{2,1,0:T(1,128)S(1)} %get-tuple-element.138), channel_id=1, source_target_pairs={{0,8},{8,16},{16,24},{1,9},{9,17},{17,25},{2,10},{10,18},{18,26},{... | collective-permute-start | bytes 3080 | tf_op jit(solution)/shard_map/ppermute | solution.py:28
  245.6 6.9 %collective-permute-start.21 = (f32[1,1,256]{2,1,0:T(1,128)S(1)}, f32[1,1,256]{2,1,0:T(1,128)S(1)}, u32[]{:S(2)}, u32[]{:S(2)}) collective-permute-start(f32[1,1,256]{2,1,0:T(1,128)S(1)} %get-tuple-element.137), channel_id=1, source_target_pairs={{8,0},{16,8},{24,16},{9,1},{17,9},{25,17},{10,2},{18,10},{26,18},{... | collective-permute-start | bytes 3080 | tf_op jit(solution)/shard_map/ppermute | solution.py:29
  246.9 6.7 %collective-permute-start.20 = (f32[1,1,256]{2,1,0:T(1,128)S(1)}, f32[1,1,256]{2,1,0:T(1,128)S(1)}, u32[]{:S(2)}, u32[]{:S(2)}) collective-permute-start(f32[1,1,256]{2,1,0:T(1,128)S(1)} %get-tuple-element.136), channel_id=1, source_target_pairs={{0,8},{8,16},{16,24},{1,9},{9,17},{17,25},{2,10},{10,18},{18,26},{... | collective-permute-start | bytes 3080 | tf_op jit(solution)/shard_map/ppermute | solution.py:28
  259.6 6.9 %collective-permute-start.25 = (f32[1,1,256]{2,1,0:T(1,128)S(1)}, f32[1,1,256]{2,1,0:T(1,128)S(1)}, u32[]{:S(2)}, u32[]{:S(2)}) collective-permute-start(f32[1,1,256]{2,1,0:T(1,128)S(1)} %get-tuple-element.135), channel_id=1, source_target_pairs={{8,0},{16,8},{24,16},{9,1},{17,9},{25,17},{10,2},{18,10},{26,18},{... | collective-permute-start | bytes 3080 | tf_op jit(solution)/shard_map/ppermute | solution.py:29
  260.9 6.8 %collective-permute-start.24 = (f32[1,1,256]{2,1,0:T(1,128)S(1)}, f32[1,1,256]{2,1,0:T(1,128)S(1)}, u32[]{:S(2)}, u32[]{:S(2)}) collective-permute-start(f32[1,1,256]{2,1,0:T(1,128)S(1)} %get-tuple-element.134), channel_id=1, source_target_pairs={{0,8},{8,16},{16,24},{1,9},{9,17},{17,25},{2,10},{10,18},{18,26},{... | collective-permute-start | bytes 3080 | tf_op jit(solution)/shard_map/ppermute | solution.py:28
  275.7 12.5 %all-to-all-start.4 = ((f32[8,4,256]{2,1,0:T(4,128)}), f32[8,4,256]{2,1,0:T(4,128)S(1)}, u32[]{:S(2)}, u32[]{:S(2)}) async-start(f32[8,4,256]{2,1,0:T(4,128)} %all_to_all.86), calls=%async_computation.4 | async-start | bytes 65536 | tf_op jit(solution)/shard_map/all_to_all | solution.py:292
  (15 other events, 163.9 us)
where the time goes:
time: 292 us; the launch traced here: 289 us
  starting transfers between devices  107 us (37%)
  blocking collectives  83.4 us (29%)
  local copies, waits for them, and re-layouts  40 us (14%)
  other arithmetic  33.7 us (12%)
  waiting for transfers between devices  19.8 us (7%)
  between operations  4.95 us (2%)
    ppermute x14, starting transfers between devices, with_halo(): before = lax.ppermute(last, axis, up)  62.1 us
    pmax x1, blocking collectives, heat_solve(): bound_high = lax.pmax(jnp.max(1.0 + off_ratio), ('gx', 'gy'))  44 us
    pmin x1, blocking collectives, heat_solve(): bound_low = lax.pmin(jnp.min(1.0 - off_ratio), ('gx', 'gy'))  39.4 us
    ppermute x14, starting transfers between devices, with_halo(): after = lax.ppermute(first, axis, down)  18.1 us
    another operation x1, local copies, waits for them, and re-layouts, per_device(): glowing.reshape(height_number_all // 2, 2, width_number // 2, 2)  9.82 us
    slice x13, local copies, waits for them, and re-layouts, with_halo(): last = lax.slice_in_dim(value, length - width, length, axis=dim)  9.32 us
    all_to_all x1, starting transfers between devices, per_device(): lax.all_to_all(updated_tile, 'gy', split_axis=0, concat_axis=1, tiled=True)  6.77 us
    concatenate x9, other arithmetic, with_halo(): value = jnp.concatenate([before, value, after], axis=dim)  6.49 us
  transfers between devices with their start and end apart: 33, of which 11 were waited for; matrix products, arithmetic and copies ran while one was open for 13% of the time, Pallas kernels for 0%

commit v1 on v0

v1 whole, which is shorter than its diff:
```python
import functools

import jax
import jax.numpy as jnp
from jax import lax
from jax.experimental import pallas as pl
from jax.experimental.pallas import tpu as pltpu
from jax.sharding import PartitionSpec as P

SR = 8
SEG = 128
SUBSTEPS = 8
HALO = 8
MESH = pl.DeviceIdType.MESH
F32 = jnp.float32


def lane_iota(shape):
    return lax.broadcasted_iota(jnp.int32, shape, 1)


def row_iota(shape):
    return lax.broadcasted_iota(jnp.int32, shape, 0)


def full_dot(a, b):
    return jnp.dot(a, b, precision=lax.Precision.HIGHEST, preferred_element_type=F32)


def kernel(
    n_gx,
    n_gy,
    shift,
    speed,
    level,
    mark,
    warm,
    store,
    film,
    bath,
    o_shift,
    o_speed,
    o_dam,
    o_warm,
    tsend,
    trecv,
    asend,
    arecv,
    pk_l,
    pk_r,
    rk_l,
    rk_r,
    rowsend,
    rowrecv,
    state,
    wt,
    tx,
    ty,
    tc,
    ac,
    fc,
    widebuf,
    gap,
    cbuf,
    crow,
    ccl,
    ccr,
    zsend,
    zrecv,
    msend,
    mrecv,
    nb_send,
    nb_recv,
    t_sem,
    a_sem,
    c_send,
    c_recv,
    z_sem,
    m_sem,
):
    ndev = n_gx * n_gy
    gx = lax.axis_index("gx")
    gy = lax.axis_index("gy")
    me = gx * n_gy + gy
    _, hh, ww = shift.shape
    rpd, _ = warm.shape
    cw = ww // 2
    ch = hh // 2
    hb = HALO // rpd
    nsl = n_gy + 2 * hb
    up = lax.rem(gx + n_gx - 1, n_gx)
    down = lax.rem(gx + 1, n_gx)
    left = lax.rem(gy + n_gy - 1, n_gy)
    right = lax.rem(gy + 1, n_gy)

    barrier = pltpu.get_barrier_semaphore()

    def greet(k, c):
        t = lax.rem(me + k, ndev)
        pl.semaphore_signal(barrier, inc=1, device_id=(t // n_gy, t % n_gy), device_id_type=MESH)
        return c

    lax.fori_loop(1, ndev, greet, 0)

    lane = lane_iota((hh, 128))
    for s in range(hh // SR):
        w8 = jnp.broadcast_to(mark[s : s + 1, :].astype(F32), (SR, ww))
        wt[HALO + SR * s : HALO + SR * s + SR, 0:ww] = w8
    w_own = wt[HALO : HALO + hh, 0:ww]
    grow = gx * hh + row_iota((hh, ww))
    gcol = gy * ww + lane_iota((hh, ww))
    dam0 = jnp.where(grow >= 1, level[0].astype(F32) * 0.125 * w_own, 1.0)
    dam1 = jnp.where(gcol >= 1, level[1].astype(F32) * 0.125 * w_own, 1.0)
    own = [shift[0], shift[1], speed[0], speed[1], dam0, dam1]
    for f in range(6):
        state[f, HALO : HALO + hh, 0:ww] = own[f]
    acc_l = jnp.zeros((hh, 128), F32)
    acc_r = jnp.zeros((hh, 128), F32)
    for f, val in enumerate(own + [w_own]):
        first, last = val[:, 0:128], val[:, ww - 128 : ww]
        here = (lane >= 8 * f) & (lane < 8 * f + 8)
        first = pltpu.roll(first, 8 * f, 1) if f else first
        acc_l = jnp.where(here, first, acc_l)
        acc_r = jnp.where(here, pltpu.roll(last, 8 * f + 8, 1), acc_r)
        if f < 6:
            rowsend[0, :, ww * f : ww * f + ww] = val[0:8, :]
            rowsend[1, :, ww * f : ww * f + ww] = val[hh - 8 : hh, :]
        else:
            rowsend[0, :, ww * f : ww * f + 128] = val[0:8, 0:128]
            rowsend[1, :, ww * f : ww * f + 128] = val[hh - 8 : hh, 0:128]
    pk_l[...] = acc_l
    pk_r[...] = acc_r

    lane_c = lane_iota((rpd, 128))

    def chunk(value, k):
        after = value[:, (cw * (k + 1)) % (cw * n_gy) :][:, 0:128]
        before = value[:, (cw * k - 128) % (cw * n_gy) :][:, 0:128]
        return value[:, cw * k : cw * k + cw], jnp.where(lane_c < 64, after, before)

    t_own = warm[...]
    base = store[...] + film[...]
    force_own = store[...] * t_own + film[...] * bath[...]
    for k in range(n_gy):
        main, edge = chunk(t_own, k)
        tsend[k, :, 0:cw] = main
        tsend[k, :, cw : cw + 128] = edge
        for q, val in enumerate((base, force_own)):
            main, edge = chunk(val, k)
            asend[k, q, :, 0:cw] = main
            asend[k, q, :, cw : cw + 128] = edge

    pl.semaphore_wait(barrier, ndev - 1)

    def remote(src, dst, ssem, rsem, where):
        return pltpu.make_async_remote_copy(
            src_ref=src, dst_ref=dst, send_sem=ssem, recv_sem=rsem, device_id=where,
            device_id_type=MESH,
        )

    def neighbours(send_l, send_r, row_u, row_d, recv_l, recv_r, got, rows, ssem, rsem):
        top, end = slice(0, 8), slice(rows - 8, rows)
        lo, mid, hi = slice(0, 8), slice(8, rows + 8), slice(rows + 8, rows + 16)
        return [
            remote(row_u, got.at[1], ssem.at[0], rsem.at[0], (up, gy)),
            remote(row_d, got.at[0], ssem.at[1], rsem.at[1], (down, gy)),
            remote(send_l, recv_r.at[mid], ssem.at[2], rsem.at[2], (gx, left)),
            remote(send_r, recv_l.at[mid], ssem.at[3], rsem.at[3], (gx, right)),
            remote(send_l.at[top], recv_r.at[hi], ssem.at[4], rsem.at[4], (up, left)),
            remote(send_r.at[top], recv_l.at[hi], ssem.at[5], rsem.at[5], (up, right)),
            remote(send_l.at[end], recv_r.at[lo], ssem.at[6], rsem.at[6], (down, left)),
            remote(send_r.at[end], recv_l.at[lo], ssem.at[7], rsem.at[7], (down, right)),
        ]

    first = neighbours(
        pk_l, pk_r, rowsend.at[0], rowsend.at[1], rk_l, rk_r, rowrecv, hh, nb_send, nb_recv
    )

    def spread_out(send, recv, sem):
        def along(k, c):
            t = lax.rem(gy + k, n_gy)
            remote(send.at[t], recv.at[gy + hb], sem.at[1], sem.at[0], (gx, t)).start()
            return c

        lax.fori_loop(1, n_gy, along, 0)
        pltpu.make_async_copy(send.at[gy], recv.at[gy + hb], sem.at[0]).start()

        @pl.when(gy < hb)
        def _():
            def go(k, c):
                remote(
                    send.at[k], recv.at[gy + hb + n_gy], sem.at[2], sem.at[0], (up, k)
                ).start()
                return c

            lax.fori_loop(0, n_gy, go, 0)

        @pl.when(gy >= n_gy - hb)
        def _():
            def go(k, c):
                remote(
                    send.at[k], recv.at[gy - (n_gy - hb)], sem.at[3], sem.at[0], (down, k)
                ).start()
                return c

            lax.fori_loop(0, n_gy, go, 0)

    def spread_sent(send, recv, sem):
        part = pl.ds(0, n_gy - 1)
        remote(send.at[part], recv.at[part], sem.at[1], sem.at[0], (gx, right)).wait_send()
        whole = pl.ds(0, n_gy)

        @pl.when(gy < hb)
        def _():
            remote(send, recv.at[whole], sem.at[2], sem.at[0], (up, gy)).wait_send()

        @pl.when(gy >= n_gy - hb)
        def _():
            remote(send, recv.at[whole], sem.at[3], sem.at[0], (down, gy)).wait_send()

    spread_out(tsend, trecv, t_sem)
    for copy in first:
        copy.start()
    spread_out(asend, arecv, a_sem)

    pltpu.make_async_copy(trecv, trecv, t_sem.at[0]).wait()
    crows = ch + 16
    for k in range(nsl):
        tc[rpd * k : rpd * k + rpd, :] = trecv[k]
    cshape = (crows, cw + 128)
    crow_i, clane_i = row_iota(cshape), lane_iota(cshape)
    t_all = tc[...]
    p = t_all
    p = jnp.where((gx == 0) & (crow_i < 8), t_all[8:9, :], p)
    p = jnp.where((gx == n_gx - 1) & (crow_i >= ch + 8), t_all[ch + 7 : ch + 8, :], p)
    wide = cw + 128
    q = jnp.where((gy == 0) & (clane_i == wide - 1), pltpu.roll(p, wide - 1, 1), p)
    q = jnp.where((gy == n_gy - 1) & (clane_i == cw), pltpu.roll(p, 1, 1), q)
    even = 0.75 * q + 0.25 * pltpu.roll(q, 1, 0)
    odd = 0.75 * q + 0.25 * pltpu.roll(q, crows - 1, 0)
    frows = hh + 2 * HALO
    need = frows // 2
    ntile = wide // 128
    for t in range(ntile):
        cols = slice(128 * t, 128 * t + 128)
        widebuf[t, pl.ds(0, need, stride=2), :] = even[4 : 4 + need, cols]
        widebuf[t, pl.ds(1, need, stride=2), :] = odd[4 : 4 + need, cols]
    r = jnp.concatenate([widebuf[t] for t in range(ntile)], axis=1)
    ecol = 0.75 * r + 0.25 * pltpu.roll(r, 1, 1)
    ocol = 0.75 * r + 0.25 * pltpu.roll(r, wide - 1, 1)
    k_i, n_i = row_iota((256, 256)), lane_iota((256, 256))
    weave = (n_i == jnp.where(k_i < 128, 2 * k_i, 2 * k_i - 255)).astype(F32)
    stack = jnp.concatenate(
        [
            jnp.concatenate([ecol[:, 128 * t : 128 * t + 128], ocol[:, 128 * t : 128 * t + 128]], 1)
            for t in range(ntile)
        ],
        axis=0,
    )
    woven = full_dot(stack, weave)
    lane_f = lane_iota((frows, 128))
    pieces = [woven[frows * t : frows * t + frows] for t in range(ntile)]
    edge = jnp.where(lane_f < 64, pieces[-1][:, 0:128], pieces[-1][:, 128:256])
    fine = jnp.concatenate(pieces[:-1] + [edge], axis=1)
    fwide = ww + 128
    tx[...] = 0.6 * (0.5 * (fine + pltpu.roll(fine, 1, 0)))
    ty[...] = 0.6 * (0.5 * (fine + pltpu.roll(fine, 1, 1)))

    for copy in first:
        copy.wait_recv()
    got_l, got_r = rk_l[...], rk_r[...]
    for f in range(7):
        from_r = pltpu.roll(got_r, 128 - 8 * f, 1) if f else got_r
        from_l = pltpu.roll(got_l, 120 - 8 * f, 1)
        side = jnp.where(lane_f < 8, from_r, jnp.where(lane_f >= 120, from_l, 0.0))
        if f == 5:
            off_l = (gy == 0) & (lane_f >= 64)
            off_r = (gy == n_gy - 1) & (lane_f < 64)
            side = jnp.where(off_l | off_r, 1.0, side)
        target = state.at[f] if f < 6 else wt
        target[:, ww:fwide] = side
        for side_row, at in ((0, 0), (1, hh + HALO)):
            if f < 6:
                target[at : at + 8, 0:ww] = rowrecv[side_row, :, ww * f : ww * f + ww]
            else:
                part = rowrecv[side_row, :, ww * f : ww * f + 128]
                for t in range(ww // 128):
                    target[at : at + 8, 128 * t : 128 * t + 128] = part

    @pl.when(gx == 0)
    def _():
        state[4, 0:8, :] = jnp.ones((8, fwide), F32)

    @pl.when(gx == n_gx - 1)
    def _():
        state[4, hh + HALO : hh + HALO + 8, :] = jnp.ones((8, fwide), F32)

    sub = row_iota((8, fwide))

    def substep(_, c):
        old = None
        for s in range(frows // 8 + 1):
            if s < frows // 8:
                rows = slice(8 * s, 8 * s + 8)
                u0, u1 = state[0, rows, :], state[1, rows, :]
                w = wt[rows, :]
                r0, r1 = pltpu.roll(u0, 1, 0), pltpu.roll(u1, 1, 0)
                p0 = jnp.where(sub == 0, old["r0"], r0) if old else r0
                p1 = jnp.where(sub == 0, old["r1"], r1) if old else r1
                open_x = u0 - p0 - tx[rows, :]
                st = jnp.maximum(open_x, 0.0)
                dx = jnp.maximum(state[4, rows, :], (1.0 - jnp.exp(st * st * -4.0)) * w)
                state[4, rows, :] = dx
                sp = 1.0 - dx
                nx = sp * open_x
                ax = sp * (u1 - p1)
                open_y = u1 - pltpu.roll(u1, 1, 1) - ty[rows, :]
                st = jnp.maximum(open_y, 0.0)
                dy = jnp.maximum(state[5, rows, :], (1.0 - jnp.exp(st * st * -4.0)) * w)
                state[5, rows, :] = dy
                sp = 1.0 - dy
                ny = sp * open_y
                ay = sp * (u0 - pltpu.roll(u0, 1, 1))
                new = dict(
                    r0=r0, r1=r1, nx=nx, ax=ax, u0=u0, u1=u1,
                    sx=pltpu.roll(nx, 7, 0), sa=pltpu.roll(ax, 7, 0),
                    fy0=pltpu.roll(ay, fwide - 1, 1) - ay,
                    fy1=pltpu.roll(ny, fwide - 1, 1) - ny,
                )
            if old:
                rows = slice(8 * s - 8, 8 * s)
                nn = jnp.where(sub == 7, new["sx"], old["sx"])
                na = jnp.where(sub == 7, new["sa"], old["sa"])
                f0 = (nn - old["nx"]) + old["fy0"]
                f1 = (na - old["ax"]) + old["fy1"]
                v0, v1 = state[2, rows, :], state[3, rows, :]
                v0 = v0 + 0.4 * (f0 - 0.05 * v0)
                v1 = v1 + 0.4 * (f1 - 0.05 * v1)
                state[2, rows, :] = v0
                state[3, rows, :] = v1
                state[0, rows, :] = old["u0"] + 0.4 * v0
                state[1, rows, :] = old["u1"] + 0.4 * v1
            old = new
        return c

    lax.fori_loop(0, SUBSTEPS, substep, 0)

    own_r = slice(HALO, HALO + hh)
    dam_x = jnp.where(grow >= 1, state[4, own_r, 0:ww], 0.0)
    dam_y = jnp.where(gcol >= 1, state[5, own_r, 0:ww], 0.0)
    both = dam_x + dam_y
    for t in range(ww // 128):
        gap[t] = both[:, 128 * t : 128 * t + 128]
    rows2 = jnp.concatenate(
        [
            gap[t, pl.ds(0, ch, stride=2), :] + gap[t, pl.ds(1, ch, stride=2), :]
            for t in range(ww // 128)
        ],
        axis=1,
    )
    k_i, n_i = row_iota((256, 128)), lane_iota((256, 128))
    pos = (k_i % SEG).astype(F32)
    col = (2 * (n_i % 64)).astype(F32)
    tab = jnp.exp(jnp.abs(pos - col) * (-4.0 / SEG)) + jnp.exp(jnp.abs(pos - col - 1.0) * (-4.0 / SEG))
    tab = jnp.where(k_i // SEG == n_i // 64, tab * (1.0 / SEG), 0.0)
    npair = ww // 256
    glow = full_dot(
        jnp.concatenate([rows2[:, 256 * t : 256 * t + 256] for t in range(npair)], axis=0), tab
    )
    resist = jnp.concatenate([glow[ch * t : ch * t + ch] for t in range(npair)], axis=1)
    cond_own = (1.0 + 0.5 * tc[8 : 8 + ch, 0:cw]) / (1.0 + resist)
    cbuf[...] = cond_own
    second = neighbours(
        cbuf.at[:, 0:128], cbuf.at[:, cw - 128 : cw], cbuf.at[0:8], cbuf.at[ch - 8 : ch],
        ccl, ccr, crow, ch, c_send, c_recv,
    )
    for copy in second:
        copy.start()

    o_shift[0] = state[0, own_r, 0:ww]
    o_shift[1] = state[1, own_r, 0:ww]
    o_speed[0] = state[2, own_r, 0:ww]
    o_speed[1] = state[3, own_r, 0:ww]
    o_dam[0] = dam_x.astype(jnp.bfloat16)
    o_dam[1] = dam_y.astype(jnp.bfloat16)

    pltpu.make_async_copy(arecv, arecv, a_sem.at[0]).wait()
    for k in range(nsl):
        ac[rpd * k : rpd * k + rpd, :] = arecv[k, 0]
        fc[rpd * k : rpd * k + rpd, :] = arecv[k, 1]

    for copy in second:
        copy.wait_recv()
    lane_k = lane_iota((crows, 128))
    cond = jnp.concatenate(
        [
            jnp.concatenate([crow[0], cbuf[...], crow[1]], axis=0),
            jnp.where(lane_k < 64, ccr[...], ccl[...]),
        ],
        axis=1,
    )
    crow_g = gx * ch - 8 + crow_i
    ccol_g = gy * cw + jnp.where(clane_i < cw + 64, clane_i, clane_i - wide)

    def four(x):
        return (
            pltpu.roll(x, 1, 0),
            pltpu.roll(x, crows - 1, 0),
            pltpu.roll(x, 1, 1),
            pltpu.roll(x, wide - 1, 1),
        )

    masks = (
        crow_g >= 1,
        crow_g <= ch * n_gx - 2,
        ccol_g >= 1,
        ccol_g <= cw * n_gy - 2,
    )
    faces = [
        jnp.where(m, 0.5 * (cond + nb), 0.0) for m, nb in zip(masks, four(cond))
    ]
    offsum = faces[0] + faces[1] + faces[2] + faces[3]
    diagonal = ac[...] + offsum
    ratio = offsum / diagonal
    peak = jnp.max(ratio[8 : 8 + ch, 0:cw])
    msend[...] = jnp.full((8, 128), peak, F32)

    def tell(k, c):
        t = lax.rem(me + k, ndev)
        remote(
            msend, mrecv.at[k - 1], m_sem.at[1], m_sem.at[0], (t // n_gy, t % n_gy)
        ).start()
        return c

    lax.fori_loop(1, ndev, tell, 0)

    t_all = tc[...]
    near = sum(f * nb for f, nb in zip(faces, four(t_all)))
    z = (fc[...] - (diagonal * t_all - near)) / diagonal
    faces = [f / diagonal for f in faces]
    for j in range(4):
        if j:
            z = z - sum(f * nb for f, nb in zip(faces, four(z)))
        for k in range(n_gy):
            zsend[k, j] = z[8 + rpd * k : 8 + rpd * k + rpd, 0:cw]

    def home(k, c):
        t = lax.rem(gy + k, n_gy)
        remote(zsend.at[t], zrecv.at[gy], z_sem.at[1], z_sem.at[0], (gx, t)).start()
        return c

    lax.fori_loop(1, n_gy, home, 0)
    pltpu.make_async_copy(zsend.at[gy], zrecv.at[gy], z_sem.at[0]).start()

    pltpu.make_async_copy(mrecv, mrecv, m_sem.at[0]).wait()
    peak = jnp.maximum(jnp.max(mrecv[...], axis=0), msend[...])[0:1, :]
    low, high = 1.0 - peak, 1.0 + peak
    center = 0.5 * (high + low)
    spread = 0.5 * (high - low)
    sigma = center / spread
    rho = 1.0 / sigma
    zero = jnp.zeros_like(center)
    e = [zero + 1.0, zero, zero, zero]
    d = [1.0 / center, zero, zero, zero]
    total = list(d)
    for _ in range(3):
        e = [e[0]] + [e[i] - d[i - 1] for i in range(1, 4)]
        rho_next = 1.0 / (2.0 * sigma - rho)
        d = [rho_next * rho * d[i] + (2.0 * rho_next / spread) * e[i] for i in range(4)]
        total = [a + b for a, b in zip(total, d)]
        rho = rho_next
    total = [jnp.concatenate([c] * (cw // 128), axis=1) for c in total]

    pltpu.make_async_copy(zrecv, zrecv, z_sem.at[0]).wait()
    for k in range(n_gy):
        x = warm[:, cw * k : cw * k + cw]
        for j in range(4):
            x = x + total[j] * zrecv[k, j]
        o_warm[:, cw * k : cw * k + cw] = x

    for copy in first + second:
        copy.wait_send()
    spread_sent(tsend, trecv, t_sem)
    spread_sent(asend, arecv, a_sem)
    part = pl.ds(0, n_gy - 1)
    remote(zsend.at[part], zrecv.at[part], z_sem.at[1], z_sem.at[0], (gx, right)).wait_send()
    remote(mrecv, mrecv, m_sem.at[1], m_sem.at[0], (gx, right)).wait_send()


def per_device(n_gx, n_gy, shift, speed, level, mark, warm, store, film, bath):
    _, hh, ww = shift.shape
    rpd, _ = warm.shape
    cw, ch = ww // 2, hh // 2
    wide, fwide = cw + 128, ww + 128
    crows, frows = ch + 16, hh + 2 * HALO
    nsl = n_gy + 2 * (HALO // rpd)
    vm = lambda *s: pltpu.VMEM(s, F32)
    dma = lambda n: pltpu.SemaphoreType.DMA((n,))
    spec = pl.BlockSpec(memory_space=pltpu.VMEM)
    return pl.pallas_call(
        functools.partial(kernel, n_gx, n_gy),
        out_shape=(
            jax.ShapeDtypeStruct(shift.shape, F32),
            jax.ShapeDtypeStruct(speed.shape, F32),
            jax.ShapeDtypeStruct(level.shape, jnp.bfloat16),
            jax.ShapeDtypeStruct(warm.shape, F32),
        ),
        in_specs=[spec] * 8,
        out_specs=(spec,) * 4,
        scratch_shapes=[
            vm(n_gy, rpd, wide),
            vm(nsl, rpd, wide),
            vm(n_gy, 2, rpd, wide),
            vm(nsl, 2, rpd, wide),
            vm(hh, 128),
            vm(hh, 128),
            vm(frows, 128),
            vm(frows, 128),
            vm(2, 8, 6 * ww + 128),
            vm(2, 8, 6 * ww + 128),
            vm(6, frows, fwide),
            vm(frows, fwide),
            vm(frows, fwide),
            vm(frows, fwide),
            vm(crows, wide),
            vm(crows, wide),
            vm(crows, wide),
            vm(wide // 128, frows, 128),
            vm(ww // 128, hh, 128),
            vm(ch, cw),
            vm(2, 8, cw),
            vm(crows, 128),
            vm(crows, 128),
            vm(n_gy, 4, rpd, cw),
            vm(n_gy, 4, rpd, cw),
            vm(8, 128),
            vm(n_gx * n_gy - 1, 8, 128),
            dma(8),
            dma(8),
            dma(4),
            dma(4),
            dma(8),
            dma(8),
            dma(2),
            dma(2),
        ],
        compiler_params=pltpu.CompilerParams(
            collective_id=0, has_side_effects=True, vmem_limit_bytes=32 * 1024 * 1024
        ),
    )(shift, speed, level, mark, warm, store, film, bath)


def solution(mesh):
    rows = P(("gx", "gy"), None)
    plate = P(None, "gx", "gy")
    return jax.shard_map(
        functools.partial(per_device, mesh.shape["gx"], mesh.shape["gy"]),
        mesh=mesh,
        in_specs=(plate, plate, plate, P("gx", "gy"), rows, rows, rows, rows),
        out_specs=(plate, plate, plate, rows),
        check_vma=False,
    )
```

time: 292 us -> 41.1 us (0.14)
  starting transfers between devices: 107 us -> 0 us
  blocking collectives: 83.4 us -> 0 us
  other arithmetic: 33.7 us -> 0 us
  local copies, waits for them, and re-layouts: 40 us -> 9.28 us
  Pallas kernels: 0 us -> 30.7 us
  waiting for transfers between devices: 19.8 us -> 0 us
  between operations: 4.95 us -> 0.65 us
    ppermute x28 -> x0, starting transfers between devices: 80.1 us -> none  [the longest x14 62.1 us: with_halo(): before = lax.ppermute(last, axis, up)]
    pmax x1 -> x0, blocking collectives: 44 us -> none  [heat_solve(): bound_high = lax.pmax(jnp.max(1.0 + off_ratio), ('gx', 'gy'))]
    pmin x1 -> x0, blocking collectives: 39.4 us -> none  [heat_solve(): bound_low = lax.pmin(jnp.min(1.0 - off_ratio), ('gx', 'gy'))]
    pallas_call x0 -> x1, Pallas kernels: none -> 30.7 us  [per_device(): pl.pallas_call(functools.partial(kernel, n_gx, n_gy), out_shape=(jax.Shap...]
    all_to_all x5 -> x0, starting transfers between devices: 26.6 us -> none  [the longest x1 6.77 us: per_device(): lax.all_to_all(updated_tile, 'gy', split_axis=0, concat_axis=1, tiled=True)]
    slice x29 -> x0, local copies, waits for them, and re-layouts: 14.2 us -> none  [the longest x13 9.32 us: with_halo(): last = lax.slice_in_dim(value, length - width, length, axis=dim)]
    all_to_all x5 -> x0, waiting for transfers between devices: 14.2 us -> none  [the longest x1 5.46 us: per_device(): lax.all_to_all(cell_warmth, 'gy', split_axis=1, concat_axis=0, tiled=True)]
    mul x37 -> x0, other arithmetic: 10.8 us -> none  [the longest x8 2.93 us: march_forward(): along_x = spring_x * shear_x]
  transfers between devices with their start and end apart: 33 -> 0, of which waited for: 11 -> 0; matrix products, arithmetic and copies ran while one was open for 13% -> 0% of each run, Pallas kernels for 0% -> 0%
where the time goes in v1:
time: 41.1 us; the launch traced here: 40.6 us
  Pallas kernels  30.7 us (75%)
  local copies, waits for them, and re-layouts  9.28 us (23%)
  between operations  0.65 us (2%)
    pallas_call x1, Pallas kernels, per_device(): pl.pallas_call(functools.partial(kernel, n_gx, n_gy), out_shape=(jax.Shap...  30.7 us
    unnamed x19, local copies, waits for them, and re-layouts  9.28 us

profile of v1, /device:TPU:0, one launch (start us, length us, event | category | flops | bytes accessed | tf_op | source)
XLA Modules:
  0.0 40.6 jit_solution(3729108142059056102)
XLA Ops:
  0.6 0.7 %copy.12.mark = s32[8,1]{1,0:T(8,128)S(1)} copy(s32[8,1]{0,1:T(1,128)} %param.11) | data formatting | bytes 64 | tf_op args[3]
  1.4 0.0 copy-start
  1.4 0.9 %copy-done = f32[2,64,512]{2,1,0:T(8,128)S(1)} copy-done((f32[2,64,512]{2,1,0:T(8,128)S(1)}, f32[2,64,512]{2,1,0:T(8,128)}, u32[]{:S(2)}) %copy-start) | copy-done | bytes 262168
  2.3 0.0 copy-start.1
  2.3 0.9 %copy-done.1 = f32[2,64,512]{2,1,0:T(8,128)S(1)} copy-done((f32[2,64,512]{2,1,0:T(8,128)S(1)}, f32[2,64,512]{2,1,0:T(8,128)}, u32[]{:S(2)}) %copy-start.1) | copy-done | bytes 262168
  3.3 0.0 copy-start.2
  3.3 0.9 %copy-done.2 = s32[2,64,512]{2,1,0:T(8,128)S(1)} copy-done((s32[2,64,512]{2,1,0:T(8,128)S(1)}, s32[2,64,512]{2,1,0:T(8,128)}, u32[]{:S(2)}) %copy-start.2) | copy-done | bytes 262168
  4.2 0.0 copy-start.3
  4.2 0.8 %copy-done.3 = f32[4,2048]{1,0:T(4,128)S(1)} copy-done((f32[4,2048]{1,0:T(4,128)S(1)}, f32[4,2048]{1,0:T(4,128)}, u32[]{:S(2)}) %copy-start.3) | copy-done | bytes 32792
  5.0 0.0 copy-start.4
  5.0 0.8 %copy-done.4 = f32[4,2048]{1,0:T(4,128)S(1)} copy-done((f32[4,2048]{1,0:T(4,128)S(1)}, f32[4,2048]{1,0:T(4,128)}, u32[]{:S(2)}) %copy-start.4) | copy-done | bytes 32792
  5.7 0.0 copy-start.5
  5.7 0.8 %copy-done.5 = f32[4,2048]{1,0:T(4,128)S(1)} copy-done((f32[4,2048]{1,0:T(4,128)S(1)}, f32[4,2048]{1,0:T(4,128)}, u32[]{:S(2)}) %copy-start.5) | copy-done | bytes 32792
  6.5 0.0 copy-start.6
  6.5 0.8 %copy-done.6 = f32[4,2048]{1,0:T(4,128)S(1)} copy-done((f32[4,2048]{1,0:T(4,128)S(1)}, f32[4,2048]{1,0:T(4,128)}, u32[]{:S(2)}) %copy-start.6) | copy-done | bytes 32792
  7.2 30.7 %shard_map.111 = (f32[2,64,512]{2,1,0:T(8,128)S(1)}, f32[2,64,512]{2,1,0:T(8,128)S(1)}, bf16[2,64,512]{2,1,0:T(8,128)(2,1)S(1)}, f32[4,2048]{1,0:T(4,128)S(1)}) custom-call(f32[2,64,512]{2,1,0:T(8,128)S(1)} %copy-done, f32[2,64,512]{2,1,0:T(8,128)S(1)} %copy-done.1, s32[2,64,512]{2,1,0:T(8,128)S(1)} %copy-done.2, s32[8,1]{1,0:T(8,128)S(1)} %copy.12.mark, ...), custom_call_target="tpu_custom_call" | custom-call | tf_op jit(solution)/shard_map/pallas_call | solution.py:500
  38.0 0.7 %copy.17 = f32[2,64,512]{2,1,0:T(8,128)} copy(f32[2,64,512]{2,1,0:T(8,128)S(1)} %get-tuple-element.8) | data formatting | bytes 524288
  38.7 0.7 %copy.18 = f32[2,64,512]{2,1,0:T(8,128)} copy(f32[2,64,512]{2,1,0:T(8,128)S(1)} %get-tuple-element.9) | data formatting | bytes 524288
  39.4 0.7 %copy.19 = bf16[2,64,512]{2,1,0:T(8,128)(2,1)} copy(bf16[2,64,512]{2,1,0:T(8,128)(2,1)S(1)} %get-tuple-element.10) | data formatting | bytes 262144
  40.0 0.6 %copy.20 = f32[4,2048]{1,0:T(4,128)} copy(f32[4,2048]{1,0:T(4,128)S(1)} %get-tuple-element.11) | data formatting | bytes 65536
Async XLA Ops:
  1.4 0.9 %copy-start = (f32[2,64,512]{2,1,0:T(8,128)S(1)}, f32[2,64,512]{2,1,0:T(8,128)}, u32[]{:S(2)}) copy-start(f32[2,64,512]{2,1,0:T(8,128)} %shift.1) | copy-start | bytes 786436
  2.3 0.9 %copy-start.1 = (f32[2,64,512]{2,1,0:T(8,128)S(1)}, f32[2,64,512]{2,1,0:T(8,128)}, u32[]{:S(2)}) copy-start(f32[2,64,512]{2,1,0:T(8,128)} %speed.1) | copy-start | bytes 786436
  3.3 0.9 %copy-start.2 = (s32[2,64,512]{2,1,0:T(8,128)S(1)}, s32[2,64,512]{2,1,0:T(8,128)}, u32[]{:S(2)}) copy-start(s32[2,64,512]{2,1,0:T(8,128)} %level.1) | copy-start | bytes 786436
  4.2 0.8 %copy-start.3 = (f32[4,2048]{1,0:T(4,128)S(1)}, f32[4,2048]{1,0:T(4,128)}, u32[]{:S(2)}) copy-start(f32[4,2048]{1,0:T(4,128)} %warm.1) | copy-start | bytes 98308
  5.0 0.8 %copy-start.4 = (f32[4,2048]{1,0:T(4,128)S(1)}, f32[4,2048]{1,0:T(4,128)}, u32[]{:S(2)}) copy-start(f32[4,2048]{1,0:T(4,128)} %store.1) | copy-start | bytes 98308
  5.7 0.8 %copy-start.5 = (f32[4,2048]{1,0:T(4,128)S(1)}, f32[4,2048]{1,0:T(4,128)}, u32[]{:S(2)}) copy-start(f32[4,2048]{1,0:T(4,128)} %film.1) | copy-start | bytes 98308
  6.5 0.8 %copy-start.6 = (f32[4,2048]{1,0:T(4,128)S(1)}, f32[4,2048]{1,0:T(4,128)}, u32[]{:S(2)}) copy-start(f32[4,2048]{1,0:T(4,128)} %bath.1) | copy-start | bytes 98308

commit v2 on v1

--- a/solution.py
+++ b/solution.py
@@ -32,12 +32,12 @@
     n_gy,
     shift,
     speed,
-    level,
+    level_h,
     mark,
-    warm,
-    store,
-    film,
-    bath,
+    warm_h,
+    store_h,
+    film_h,
+    bath_h,
     o_shift,
     o_speed,
     o_dam,
@@ -50,8 +50,13 @@
     pk_r,
     rk_l,
     rk_r,
-    rowsend,
-    rowrecv,
+    wsend,
+    wrecv,
+    level,
+    warm,
+    store,
+    film,
+    bath,
     state,
     wt,
     tx,
@@ -77,13 +82,17 @@
     c_recv,
     z_sem,
     m_sem,
+    in_sem,
+    dambuf,
+    warmbuf,
+    out_sem,
 ):
     ndev = n_gx * n_gy
     gx = lax.axis_index("gx")
     gy = lax.axis_index("gy")
     me = gx * n_gy + gy
     _, hh, ww = shift.shape
-    rpd, _ = warm.shape
+    rpd, _ = warm_h.shape
     cw = ww // 2
     ch = hh // 2
     hb = HALO // rpd
@@ -93,6 +102,23 @@
     left = lax.rem(gy + n_gy - 1, n_gy)
     right = lax.rem(gy + 1, n_gy)
 
+    own_r = slice(HALO, HALO + hh)
+    loads = [
+        pltpu.make_async_copy(src, dst, in_sem.at[i])
+        for i, (src, dst) in enumerate(
+            (
+                (warm_h, warm),
+                (level_h, level),
+                (shift, state.at[0:2, own_r, 0:ww]),
+                (speed, state.at[2:4, own_r, 0:ww]),
+                (store_h, store),
+                (film_h, film),
+                (bath_h, bath),
+            )
+        )
+    ]
+    for copy in loads:
+        copy.start()
     barrier = pltpu.get_barrier_semaphore()
 
     def greet(k, c):
@@ -104,30 +130,26 @@
 
     lane = lane_iota((hh, 128))
     for s in range(hh // SR):
-        w8 = jnp.broadcast_to(mark[s : s + 1, :].astype(F32), (SR, ww))
-        wt[HALO + SR * s : HALO + SR * s + SR, 0:ww] = w8
-    w_own = wt[HALO : HALO + hh, 0:ww]
+        wt[HALO + SR * s : HALO + SR * s + SR, 0:ww] = jnp.full((SR, ww), mark[0, s], jnp.int32).astype(F32)
+    w_own = wt[own_r, 0:ww]
     grow = gx * hh + row_iota((hh, ww))
     gcol = gy * ww + lane_iota((hh, ww))
-    dam0 = jnp.where(grow >= 1, level[0].astype(F32) * 0.125 * w_own, 1.0)
-    dam1 = jnp.where(gcol >= 1, level[1].astype(F32) * 0.125 * w_own, 1.0)
-    own = [shift[0], shift[1], speed[0], speed[1], dam0, dam1]
-    for f in range(6):
-        state[f, HALO : HALO + hh, 0:ww] = own[f]
+    loads[1].wait()
+    state[4, own_r, 0:ww] = jnp.where(grow >= 1, level[0].astype(F32) * 0.125 * w_own, 1.0)
+    state[5, own_r, 0:ww] = jnp.where(gcol >= 1, level[1].astype(F32) * 0.125 * w_own, 1.0)
+    wsend[0] = wt[HALO : HALO + 8, 0:128]
+    wsend[1] = wt[HALO + hh - 8 : HALO + hh, 0:128]
+    loads[2].wait()
+    loads[3].wait()
     acc_l = jnp.zeros((hh, 128), F32)
     acc_r = jnp.zeros((hh, 128), F32)
-    for f, val in enumerate(own + [w_own]):
-        first, last = val[:, 0:128], val[:, ww - 128 : ww]
+    for f in range(7):
+        field = state.at[f] if f < 6 else wt
+        first, last = field[own_r, 0:128], field[own_r, ww - 128 : ww]
         here = (lane >= 8 * f) & (lane < 8 * f + 8)
         first = pltpu.roll(first, 8 * f, 1) if f else first
         acc_l = jnp.where(here, first, acc_l)
         acc_r = jnp.where(here, pltpu.roll(last, 8 * f + 8, 1), acc_r)
-        if f < 6:
-            rowsend[0, :, ww * f : ww * f + ww] = val[0:8, :]
-            rowsend[1, :, ww * f : ww * f + ww] = val[hh - 8 : hh, :]
-        else:
-            rowsend[0, :, ww * f : ww * f + 128] = val[0:8, 0:128]
-            rowsend[1, :, ww * f : ww * f + 128] = val[hh - 8 : hh, 0:128]
     pk_l[...] = acc_l
     pk_r[...] = acc_r
 
@@ -138,6 +160,8 @@
         before = value[:, (cw * k - 128) % (cw * n_gy) :][:, 0:128]
         return value[:, cw * k : cw * k + cw], jnp.where(lane_c < 64, after, before)
 
+    for i in (0, 4, 5, 6):
+        loads[i].wait()
     t_own = warm[...]
     base = store[...] + film[...]
     force_own = store[...] * t_own + film[...] * bath[...]
@@ -158,12 +182,12 @@
             device_id_type=MESH,
         )
 
-    def neighbours(send_l, send_r, row_u, row_d, recv_l, recv_r, got, rows, ssem, rsem):
+    def neighbours(send_l, send_r, row_u, row_d, recv_l, recv_r, got_u, got_d, rows, ssem, rsem):
         top, end = slice(0, 8), slice(rows - 8, rows)
         lo, mid, hi = slice(0, 8), slice(8, rows + 8), slice(rows + 8, rows + 16)
         return [
-            remote(row_u, got.at[1], ssem.at[0], rsem.at[0], (up, gy)),
-            remote(row_d, got.at[0], ssem.at[1], rsem.at[1], (down, gy)),
+            remote(row_u, got_d, ssem.at[0], rsem.at[0], (up, gy)),
+            remote(row_d, got_u, ssem.at[1], rsem.at[1], (down, gy)),
             remote(send_l, recv_r.at[mid], ssem.at[2], rsem.at[2], (gx, left)),
             remote(send_r, recv_l.at[mid], ssem.at[3], rsem.at[3], (gx, right)),
             remote(send_l.at[top], recv_r.at[hi], ssem.at[4], rsem.at[4], (up, left)),
@@ -173,8 +197,21 @@
         ]
 
     first = neighbours(
-        pk_l, pk_r, rowsend.at[0], rowsend.at[1], rk_l, rk_r, rowrecv, hh, nb_send, nb_recv
-    )
+        pk_l,
+        pk_r,
+        state.at[:, HALO : HALO + 8, 0:ww],
+        state.at[:, HALO + hh - 8 : HALO + hh, 0:ww],
+        rk_l,
+        rk_r,
+        state.at[:, 0:8, 0:ww],
+        state.at[:, HALO + hh : HALO + hh + 8, 0:ww],
+        hh,
+        nb_send,
+        nb_recv,
+    ) + [
+        remote(wsend.at[0], wrecv.at[1], nb_send.at[8], nb_recv.at[8], (up, gy)),
+        remote(wsend.at[1], wrecv.at[0], nb_send.at[9], nb_recv.at[9], (down, gy)),
+    ]
 
     def spread_out(send, recv, sem):
         def along(k, c):
@@ -279,13 +316,9 @@
             side = jnp.where(off_l | off_r, 1.0, side)
         target = state.at[f] if f < 6 else wt
         target[:, ww:fwide] = side
-        for side_row, at in ((0, 0), (1, hh + HALO)):
-            if f < 6:
-                target[at : at + 8, 0:ww] = rowrecv[side_row, :, ww * f : ww * f + ww]
-            else:
-                part = rowrecv[side_row, :, ww * f : ww * f + 128]
-                for t in range(ww // 128):
-                    target[at : at + 8, 128 * t : 128 * t + 128] = part
+    for side_row, at in ((0, 0), (1, hh + HALO)):
+        for t in range(ww // 128):
+            wt[at : at + 8, 128 * t : 128 * t + 128] = wrecv[side_row]
 
     @pl.when(gx == 0)
     def _():
@@ -294,6 +327,9 @@
     @pl.when(gx == n_gx - 1)
     def _():
         state[4, hh + HALO : hh + HALO + 8, :] = jnp.ones((8, fwide), F32)
+
+    for copy in first:
+        copy.wait_send()
 
     sub = row_iota((8, fwide))
 
@@ -345,7 +381,6 @@
 
     lax.fori_loop(0, SUBSTEPS, substep, 0)
 
-    own_r = slice(HALO, HALO + hh)
     dam_x = jnp.where(grow >= 1, state[4, own_r, 0:ww], 0.0)
     dam_y = jnp.where(gcol >= 1, state[5, own_r, 0:ww], 0.0)
     both = dam_x + dam_y
@@ -372,17 +407,26 @@
     cbuf[...] = cond_own
     second = neighbours(
         cbuf.at[:, 0:128], cbuf.at[:, cw - 128 : cw], cbuf.at[0:8], cbuf.at[ch - 8 : ch],
-        ccl, ccr, crow, ch, c_send, c_recv,
+        ccl, ccr, crow.at[0], crow.at[1], ch, c_send, c_recv,
     )
     for copy in second:
         copy.start()
 
-    o_shift[0] = state[0, own_r, 0:ww]
-    o_shift[1] = state[1, own_r, 0:ww]
-    o_speed[0] = state[2, own_r, 0:ww]
-    o_speed[1] = state[3, own_r, 0:ww]
-    o_dam[0] = dam_x.astype(jnp.bfloat16)
-    o_dam[1] = dam_y.astype(jnp.bfloat16)
+    dambuf[0] = dam_x.astype(jnp.bfloat16)
+    dambuf[1] = dam_y.astype(jnp.bfloat16)
+    puts = [
+        pltpu.make_async_copy(src, dst, out_sem.at[i])
+        for i, (src, dst) in enumerate(
+            (
+                (state.at[0:2, own_r, 0:ww], o_shift),
+                (state.at[2:4, own_r, 0:ww], o_speed),
+                (dambuf, o_dam),
+                (warmbuf, o_warm),
+            )
+        )
+    ]
+    for copy in puts[0:3]:
+        copy.start()
 
     pltpu.make_async_copy(arecv, arecv, a_sem.at[0]).wait()
     for k in range(nsl):
@@ -476,15 +520,31 @@
         x = warm[:, cw * k : cw * k + cw]
         for j in range(4):
             x = x + total[j] * zrecv[k, j]
-        o_warm[:, cw * k : cw * k + cw] = x
-
-    for copy in first + second:
+        warmbuf[:, cw * k : cw * k + cw] = x
+    puts[3].start()
+
+    for copy in second:
         copy.wait_send()
     spread_sent(tsend, trecv, t_sem)
     spread_sent(asend, arecv, a_sem)
     part = pl.ds(0, n_gy - 1)
     remote(zsend.at[part], zrecv.at[part], z_sem.at[1], z_sem.at[0], (gx, right)).wait_send()
     remote(mrecv, mrecv, m_sem.at[1], m_sem.at[0], (gx, right)).wait_send()
+    for copy in puts:
+        copy.wait()
+
+
+def put_out(*refs):
+    src, dst, via, (isem, osem) = refs[0:4], refs[4:8], refs[8:12], refs[12:14]
+    into = [pltpu.make_async_copy(src[i], via[i], isem.at[i]) for i in range(4)]
+    out = [pltpu.make_async_copy(via[i], dst[i], osem.at[i]) for i in range(4)]
+    for copy in into:
+        copy.start()
+    for i in range(4):
+        into[i].wait()
+        out[i].start()
+    for copy in out:
+        copy.wait()
 
 
 def per_device(n_gx, n_gy, shift, speed, level, mark, warm, store, film, bath):
@@ -496,8 +556,8 @@
     nsl = n_gy + 2 * (HALO // rpd)
     vm = lambda *s: pltpu.VMEM(s, F32)
     dma = lambda n: pltpu.SemaphoreType.DMA((n,))
-    spec = pl.BlockSpec(memory_space=pltpu.VMEM)
-    return pl.pallas_call(
+    hbm = pl.BlockSpec(memory_space=pltpu.HBM)
+    outs = pl.pallas_call(
         functools.partial(kernel, n_gx, n_gy),
         out_shape=(
             jax.ShapeDtypeStruct(shift.shape, F32),
@@ -505,8 +565,8 @@
             jax.ShapeDtypeStruct(level.shape, jnp.bfloat16),
             jax.ShapeDtypeStruct(warm.shape, F32),
         ),
-        in_specs=[spec] * 8,
-        out_specs=(spec,) * 4,
+        in_specs=[hbm] * 3 + [pl.BlockSpec(memory_space=pltpu.SMEM)] + [hbm] * 4,
+        out_specs=(hbm,) * 4,
         scratch_shapes=[
             vm(n_gy, rpd, wide),
             vm(nsl, rpd, wide),
@@ -516,8 +576,13 @@
             vm(hh, 128),
             vm(frows, 128),
             vm(frows, 128),
-            vm(2, 8, 6 * ww + 128),
-            vm(2, 8, 6 * ww + 128),
+            vm(2, 8, 128),
+            vm(2, 8, 128),
+            pltpu.VMEM(level.shape, level.dtype),
+            vm(*warm.shape),
+            vm(*warm.shape),
+            vm(*warm.shape),
+            vm(*warm.shape),
             vm(6, frows, fwide),
             vm(frows, fwide),
             vm(frows, fwide),
@@ -535,19 +600,30 @@
             vm(n_gy, 4, rpd, cw),
             vm(8, 128),
             vm(n_gx * n_gy - 1, 8, 128),
-            dma(8),
-            dma(8),
+            dma(10),
+            dma(10),
             dma(4),
             dma(4),
             dma(8),
             dma(8),
             dma(2),
             dma(2),
+            dma(7),
+            pltpu.VMEM(level.shape, jnp.bfloat16),
+            vm(*warm.shape),
+            dma(4),
         ],
         compiler_params=pltpu.CompilerParams(
-            collective_id=0, has_side_effects=True, vmem_limit_bytes=32 * 1024 * 1024
+            collective_id=0, has_side_effects=True
         ),
-    )(shift, speed, level, mark, warm, store, film, bath)
+    )(shift, speed, level, mark.reshape(1, hh // SR), warm, store, film, bath)
+    return pl.pallas_call(
+        put_out,
+        out_shape=tuple(jax.ShapeDtypeStruct(o.shape, o.dtype) for o in outs),
+        in_specs=[hbm] * 4,
+        out_specs=(hbm,) * 4,
+        scratch_shapes=[pltpu.VMEM(o.shape, o.dtype) for o in outs] + [dma(4), dma(4)],
+    )(*outs)
 
 
 def solution(mesh):

time: 41.1 us -> 35.2 us (0.86)
  local copies, waits for them, and re-layouts: 9.28 us -> 0 us
  Pallas kernels: 30.7 us -> 34.4 us
    unnamed x19 -> x0, local copies, waits for them, and re-layouts: 9.28 us -> none
    pallas_call x0 -> x1, Pallas kernels: none -> 1.85 us  [per_device(): pl.pallas_call(put_out, out_shape=tuple((jax.ShapeDtypeStruct(o.shape, o....]
    pallas_call x1, Pallas kernels: 30.7 us -> 32.5 us  [per_device(): pl.pallas_call(functools.partial(kernel, n_gx, n_gy), out_shape=(jax.Shap...]
where the time goes in v2:
time: 35.2 us; the launch traced here: 35 us
  Pallas kernels  34.4 us (98%)
  between operations  0.64 us (2%)
    pallas_call x1, Pallas kernels, per_device(): pl.pallas_call(functools.partial(kernel, n_gx, n_gy), out_shape=(jax.Shap...  32.5 us
    pallas_call x1, Pallas kernels, per_device(): pl.pallas_call(put_out, out_shape=tuple((jax.ShapeDtypeStruct(o.shape, o....  1.85 us

profile of v2, /device:TPU:0, one launch (start us, length us, event | category | flops | bytes accessed | tf_op | source)
XLA Modules:
  0.0 35.0 jit_solution(16954876577854442528)
XLA Ops:
  0.6 32.5 %shard_map.111 = (f32[2,64,512]{2,1,0:T(8,128)}, f32[2,64,512]{2,1,0:T(8,128)}, bf16[2,64,512]{2,1,0:T(8,128)(2,1)}, f32[4,2048]{1,0:T(4,128)}) custom-call(f32[2,64,512]{2,1,0:T(8,128)} %shift.1, f32[2,64,512]{2,1,0:T(8,128)} %speed.1, s32[2,64,512]{2,1,0:T(8,128)} %level_h.1, s32[1,8]{1,0:T(1,128)} %bitcast.1, f32[4,2048]{1,0:T(4,128)} %warm_h.1, ...), custom_call_target="tpu_custom_call" | custom-call | tf_op jit(solution)/shard_map/pallas_call | solution.py:560
  33.2 1.9 %shard_map.112 = (f32[2,64,512]{2,1,0:T(8,128)}, f32[2,64,512]{2,1,0:T(8,128)}, bf16[2,64,512]{2,1,0:T(8,128)(2,1)}, f32[4,2048]{1,0:T(4,128)}) custom-call(f32[2,64,512]{2,1,0:T(8,128)} %get-tuple-element.8.refs_0_, f32[2,64,512]{2,1,0:T(8,128)} %get-tuple-element.9.refs_1_, bf16[2,64,512]{2,1,0:T(8,128)(2,1)} %get-tuple-element.10.refs_2_, ...), custom_call_target="tpu_custom_call" | custom-call | tf_op jit(solution)/shard_map/pallas_call | solution.py:620

commit v3 on v2

--- a/solution.py
+++ b/solution.py
@@ -52,6 +52,10 @@
     rk_r,
     wsend,
     wrecv,
+    rowsend,
+    rowrecv,
+    keep,
+    hist,
     level,
     warm,
     store,
@@ -150,6 +154,9 @@
         first = pltpu.roll(first, 8 * f, 1) if f else first
         acc_l = jnp.where(here, first, acc_l)
         acc_r = jnp.where(here, pltpu.roll(last, 8 * f + 8, 1), acc_r)
+        if f < 6:
+            rowsend[0, f] = field[HALO : HALO + 8, 0:ww]
+            rowsend[1, f] = field[HALO + hh - 8 : HALO + hh, 0:ww]
     pk_l[...] = acc_l
     pk_r[...] = acc_r
 
@@ -199,12 +206,12 @@
     first = neighbours(
         pk_l,
         pk_r,
-        state.at[:, HALO : HALO + 8, 0:ww],
-        state.at[:, HALO + hh - 8 : HALO + hh, 0:ww],
+        rowsend.at[0],
+        rowsend.at[1],
         rk_l,
         rk_r,
-        state.at[:, 0:8, 0:ww],
-        state.at[:, HALO + hh : HALO + hh + 8, 0:ww],
+        rowrecv.at[0],
+        rowrecv.at[1],
         hh,
         nb_send,
         nb_recv,
@@ -258,9 +265,9 @@
     spread_out(tsend, trecv, t_sem)
     for copy in first:
         copy.start()
+
+    pltpu.make_async_copy(trecv, trecv, t_sem.at[0]).wait()
     spread_out(asend, arecv, a_sem)
-
-    pltpu.make_async_copy(trecv, trecv, t_sem.at[0]).wait()
     crows = ch + 16
     for k in range(nsl):
         tc[rpd * k : rpd * k + rpd, :] = trecv[k]
@@ -303,7 +310,7 @@
     tx[...] = 0.6 * (0.5 * (fine + pltpu.roll(fine, 1, 0)))
     ty[...] = 0.6 * (0.5 * (fine + pltpu.roll(fine, 1, 1)))
 
-    for copy in first:
+    for copy in first[2:8]:
         copy.wait_recv()
     got_l, got_r = rk_l[...], rk_r[...]
     for f in range(7):
@@ -316,7 +323,79 @@
             side = jnp.where(off_l | off_r, 1.0, side)
         target = state.at[f] if f < 6 else wt
         target[:, ww:fwide] = side
+    sub = row_iota((8, fwide))
+    last_strip = frows // 8 - 1
+
+    def edges(s, old):
+        rows = slice(8 * s, 8 * s + 8)
+        u0, u1 = state[0, rows, :], state[1, rows, :]
+        w = wt[rows, :]
+        r0, r1 = pltpu.roll(u0, 1, 0), pltpu.roll(u1, 1, 0)
+        p0 = jnp.where(sub == 0, old["r0"], r0) if old else r0
+        p1 = jnp.where(sub == 0, old["r1"], r1) if old else r1
+        open_x = u0 - p0 - tx[rows, :]
+        st = jnp.maximum(open_x, 0.0)
+        dx = jnp.maximum(state[4, rows, :], (1.0 - jnp.exp(st * st * -4.0)) * w)
+        state[4, rows, :] = dx
+        sp = 1.0 - dx
+        nx = sp * open_x
+        ax = sp * (u1 - p1)
+        open_y = u1 - pltpu.roll(u1, 1, 1) - ty[rows, :]
+        st = jnp.maximum(open_y, 0.0)
+        dy = jnp.maximum(state[5, rows, :], (1.0 - jnp.exp(st * st * -4.0)) * w)
+        state[5, rows, :] = dy
+        sp = 1.0 - dy
+        ny = sp * open_y
+        ay = sp * (u0 - pltpu.roll(u0, 1, 1))
+        return dict(
+            r0=r0, r1=r1, nx=nx, ax=ax, u0=u0, u1=u1,
+            sx=pltpu.roll(nx, 7, 0), sa=pltpu.roll(ax, 7, 0),
+            fy0=pltpu.roll(ay, fwide - 1, 1) - ay,
+            fy1=pltpu.roll(ny, fwide - 1, 1) - ny,
+        )
+
+    def advance(s, old, new):
+        rows = slice(8 * s, 8 * s + 8)
+        nn = jnp.where(sub == 7, new["sx"], old["sx"])
+        na = jnp.where(sub == 7, new["sa"], old["sa"])
+        f0 = (nn - old["nx"]) + old["fy0"]
+        f1 = (na - old["ax"]) + old["fy1"]
+        v0, v1 = state[2, rows, :], state[3, rows, :]
+        v0 = v0 + 0.4 * (f0 - 0.05 * v0)
+        v1 = v1 + 0.4 * (f1 - 0.05 * v1)
+        state[2, rows, :] = v0
+        state[3, rows, :] = v1
+        state[0, rows, :] = old["u0"] + 0.4 * v0
+        state[1, rows, :] = old["u1"] + 0.4 * v1
+
+    redo = (slice(8, 16), slice(8 * last_strip - 8, 8 * last_strip))
+    for i, rows in enumerate(redo):
+        keep[i] = state[:, rows, :]
+
+    def interior(t, c):
+        old = None
+        for s in range(1, last_strip):
+            new = edges(s, old)
+            if s == 2:
+                hist[t, 0] = new["sx"]
+                hist[t, 1] = new["sa"]
+            if s == last_strip - 2:
+                hist[t, 2] = new["r0"]
+                hist[t, 3] = new["r1"]
+            if old:
+                advance(s - 1, old, new)
+            old = new
+        advance(last_strip - 1, old, old)
+        return c
+
+    lax.fori_loop(0, SUBSTEPS, interior, 0)
+
+    for copy in first[0:2] + first[8:10]:
+        copy.wait_recv()
+    for i, rows in enumerate(redo):
+        state[:, rows, :] = keep[i]
     for side_row, at in ((0, 0), (1, hh + HALO)):
+        state[:, at : at + 8, 0:ww] = rowrecv[side_row]
         for t in range(ww // 128):
             wt[at : at + 8, 128 * t : 128 * t + 128] = wrecv[side_row]
 
@@ -328,58 +407,18 @@
     def _():
         state[4, hh + HALO : hh + HALO + 8, :] = jnp.ones((8, fwide), F32)
 
-    for copy in first:
-        copy.wait_send()
-
-    sub = row_iota((8, fwide))
-
-    def substep(_, c):
-        old = None
-        for s in range(frows // 8 + 1):
-            if s < frows // 8:
-                rows = slice(8 * s, 8 * s + 8)
-                u0, u1 = state[0, rows, :], state[1, rows, :]
-                w = wt[rows, :]
-                r0, r1 = pltpu.roll(u0, 1, 0), pltpu.roll(u1, 1, 0)
-                p0 = jnp.where(sub == 0, old["r0"], r0) if old else r0
-                p1 = jnp.where(sub == 0, old["r1"], r1) if old else r1
-                open_x = u0 - p0 - tx[rows, :]
-                st = jnp.maximum(open_x, 0.0)
-                dx = jnp.maximum(state[4, rows, :], (1.0 - jnp.exp(st * st * -4.0)) * w)
-                state[4, rows, :] = dx
-                sp = 1.0 - dx
-                nx = sp * open_x
-                ax = sp * (u1 - p1)
-                open_y = u1 - pltpu.roll(u1, 1, 1) - ty[rows, :]
-                st = jnp.maximum(open_y, 0.0)
-                dy = jnp.maximum(state[5, rows, :], (1.0 - jnp.exp(st * st * -4.0)) * w)
-                state[5, rows, :] = dy
-                sp = 1.0 - dy
-                ny = sp * open_y
-                ay = sp * (u0 - pltpu.roll(u0, 1, 1))
-                new = dict(
-                    r0=r0, r1=r1, nx=nx, ax=ax, u0=u0, u1=u1,
-                    sx=pltpu.roll(nx, 7, 0), sa=pltpu.roll(ax, 7, 0),
-                    fy0=pltpu.roll(ay, fwide - 1, 1) - ay,
-                    fy1=pltpu.roll(ny, fwide - 1, 1) - ny,
-                )
-            if old:
-                rows = slice(8 * s - 8, 8 * s)
-                nn = jnp.where(sub == 7, new["sx"], old["sx"])
-                na = jnp.where(sub == 7, new["sa"], old["sa"])
-                f0 = (nn - old["nx"]) + old["fy0"]
-                f1 = (na - old["ax"]) + old["fy1"]
-                v0, v1 = state[2, rows, :], state[3, rows, :]
-                v0 = v0 + 0.4 * (f0 - 0.05 * v0)
-                v1 = v1 + 0.4 * (f1 - 0.05 * v1)
-                state[2, rows, :] = v0
-                state[3, rows, :] = v1
-                state[0, rows, :] = old["u0"] + 0.4 * v0
-                state[1, rows, :] = old["u1"] + 0.4 * v1
-            old = new
+    def border(t, c):
+        e0 = edges(0, None)
+        e1 = edges(1, e0)
+        advance(0, e0, e1)
+        advance(1, e1, dict(sx=hist[t, 0], sa=hist[t, 1]))
+        e8 = edges(last_strip - 1, dict(r0=hist[t, 2], r1=hist[t, 3]))
+        e9 = edges(last_strip, e8)
+        advance(last_strip - 1, e8, e9)
+        advance(last_strip, e9, e9)
         return c
 
-    lax.fori_loop(0, SUBSTEPS, substep, 0)
+    lax.fori_loop(0, SUBSTEPS, border, 0)
 
     dam_x = jnp.where(grow >= 1, state[4, own_r, 0:ww], 0.0)
     dam_y = jnp.where(gcol >= 1, state[5, own_r, 0:ww], 0.0)
@@ -523,7 +562,7 @@
         warmbuf[:, cw * k : cw * k + cw] = x
     puts[3].start()
 
-    for copy in second:
+    for copy in first + second:
         copy.wait_send()
     spread_sent(tsend, trecv, t_sem)
     spread_sent(asend, arecv, a_sem)
@@ -578,6 +617,10 @@
             vm(frows, 128),
             vm(2, 8, 128),
             vm(2, 8, 128),
+            vm(2, 6, 8, ww),
+            vm(2, 6, 8, ww),
+            vm(2, 6, 8, fwide),
+            vm(SUBSTEPS, 4, 8, fwide),
             pltpu.VMEM(level.shape, level.dtype),
             vm(*warm.shape),
             vm(*warm.shape),

time: 35.2 us -> 35.1 us (level)
  no operation moved by 1% of the time
where the time goes in v3:
time: 35.1 us; the launch traced here: 34.9 us
  Pallas kernels  34.3 us (98%)
  between operations  0.64 us (2%)
    pallas_call x1, Pallas kernels, per_device(): pl.pallas_call(functools.partial(kernel, n_gx, n_gy), out_shape=(jax.Shap...  32.4 us
    pallas_call x1, Pallas kernels, per_device(): pl.pallas_call(put_out, out_shape=tuple((jax.ShapeDtypeStruct(o.shape, o....  1.85 us

profile of v3, /device:TPU:0, one launch (start us, length us, event | category | flops | bytes accessed | tf_op | source)
XLA Modules:
  0.0 34.9 jit_solution(10552990116822885299)
XLA Ops:
  0.6 32.4 %shard_map.111 = (f32[2,64,512]{2,1,0:T(8,128)}, f32[2,64,512]{2,1,0:T(8,128)}, bf16[2,64,512]{2,1,0:T(8,128)(2,1)}, f32[4,2048]{1,0:T(4,128)}) custom-call(f32[2,64,512]{2,1,0:T(8,128)} %shift.1, f32[2,64,512]{2,1,0:T(8,128)} %speed.1, s32[2,64,512]{2,1,0:T(8,128)} %level_h.1, s32[1,8]{1,0:T(1,128)} %bitcast.1, f32[4,2048]{1,0:T(4,128)} %warm_h.1, ...), custom_call_target="tpu_custom_call" | custom-call | tf_op jit(solution)/shard_map/pallas_call | solution.py:599
  33.1 1.9 %shard_map.112 = (f32[2,64,512]{2,1,0:T(8,128)}, f32[2,64,512]{2,1,0:T(8,128)}, bf16[2,64,512]{2,1,0:T(8,128)(2,1)}, f32[4,2048]{1,0:T(4,128)}) custom-call(f32[2,64,512]{2,1,0:T(8,128)} %get-tuple-element.8.refs_0_, f32[2,64,512]{2,1,0:T(8,128)} %get-tuple-element.9.refs_1_, bf16[2,64,512]{2,1,0:T(8,128)(2,1)} %get-tuple-element.10.refs_2_, ...), custom_call_target="tpu_custom_call" | custom-call | tf_op jit(solution)/shard_map/pallas_call | solution.py:663

commit v4 on v3

--- a/solution.py
+++ b/solution.py
@@ -66,8 +66,7 @@
     tx,
     ty,
     tc,
-    ac,
-    fc,
+    acf,
     widebuf,
     gap,
     cbuf,
@@ -267,7 +266,14 @@
         copy.start()
 
     pltpu.make_async_copy(trecv, trecv, t_sem.at[0]).wait()
-    spread_out(asend, arecv, a_sem)
+
+    def late(k, c):
+        t = lax.rem(gy + k, n_gy)
+        remote(asend.at[t], arecv.at[gy], a_sem.at[1], a_sem.at[0], (gx, t)).start()
+        return c
+
+    lax.fori_loop(1, n_gy, late, 0)
+    pltpu.make_async_copy(asend.at[gy], arecv.at[gy], a_sem.at[0]).start()
     crows = ch + 16
     for k in range(nsl):
         tc[rpd * k : rpd * k + rpd, :] = trecv[k]
@@ -390,6 +396,19 @@
 
     lax.fori_loop(0, SUBSTEPS, interior, 0)
 
+    pltpu.make_async_copy(arecv, arecv, a_sem.at[0]).wait()
+    for k in range(n_gy):
+        for q in range(2):
+            acf[q, 8 + rpd * k : 8 + rpd * k + rpd, :] = arecv[k, q]
+    coarse_rows = [
+        remote(
+            acf.at[:, 8:16], acf.at[:, ch + 8 : ch + 16], a_sem.at[2], a_sem.at[4], (up, gy)
+        ),
+        remote(acf.at[:, ch : ch + 8], acf.at[:, 0:8], a_sem.at[3], a_sem.at[5], (down, gy)),
+    ]
+    for copy in coarse_rows:
+        copy.start()
+
     for copy in first[0:2] + first[8:10]:
         copy.wait_recv()
     for i, rows in enumerate(redo):
@@ -467,10 +486,8 @@
     for copy in puts[0:3]:
         copy.start()
 
-    pltpu.make_async_copy(arecv, arecv, a_sem.at[0]).wait()
-    for k in range(nsl):
-        ac[rpd * k : rpd * k + rpd, :] = arecv[k, 0]
-        fc[rpd * k : rpd * k + rpd, :] = arecv[k, 1]
+    for copy in coarse_rows:
+        copy.wait_recv()
 
     for copy in second:
         copy.wait_recv()
@@ -503,7 +520,7 @@
         jnp.where(m, 0.5 * (cond + nb), 0.0) for m, nb in zip(masks, four(cond))
     ]
     offsum = faces[0] + faces[1] + faces[2] + faces[3]
-    diagonal = ac[...] + offsum
+    diagonal = acf[0] + offsum
     ratio = offsum / diagonal
     peak = jnp.max(ratio[8 : 8 + ch, 0:cw])
     msend[...] = jnp.full((8, 128), peak, F32)
@@ -519,7 +536,7 @@
 
     t_all = tc[...]
     near = sum(f * nb for f, nb in zip(faces, four(t_all)))
-    z = (fc[...] - (diagonal * t_all - near)) / diagonal
+    z = (acf[1] - (diagonal * t_all - near)) / diagonal
     faces = [f / diagonal for f in faces]
     for j in range(4):
         if j:
@@ -565,7 +582,12 @@
     for copy in first + second:
         copy.wait_send()
     spread_sent(tsend, trecv, t_sem)
-    spread_sent(asend, arecv, a_sem)
+    remote(
+        asend.at[pl.ds(0, n_gy - 1)], arecv.at[pl.ds(0, n_gy - 1)], a_sem.at[1], a_sem.at[0],
+        (gx, right),
+    ).wait_send()
+    for copy in coarse_rows:
+        copy.wait_send()
     part = pl.ds(0, n_gy - 1)
     remote(zsend.at[part], zrecv.at[part], z_sem.at[1], z_sem.at[0], (gx, right)).wait_send()
     remote(mrecv, mrecv, m_sem.at[1], m_sem.at[0], (gx, right)).wait_send()
@@ -610,7 +632,7 @@
             vm(n_gy, rpd, wide),
             vm(nsl, rpd, wide),
             vm(n_gy, 2, rpd, wide),
-            vm(nsl, 2, rpd, wide),
+            vm(n_gy, 2, rpd, wide),
             vm(hh, 128),
             vm(hh, 128),
             vm(frows, 128),
@@ -631,8 +653,7 @@
             vm(frows, fwide),
             vm(frows, fwide),
             vm(crows, wide),
-            vm(crows, wide),
-            vm(crows, wide),
+            vm(2, crows, wide),
             vm(wide // 128, frows, 128),
             vm(ww // 128, hh, 128),
             vm(ch, cw),
@@ -646,7 +667,7 @@
             dma(10),
             dma(10),
             dma(4),
-            dma(4),
+            dma(6),
             dma(8),
             dma(8),
             dma(2),

time: 35.1 us -> 35.1 us (level)
  no operation moved by 1% of the time
where the time goes in v4:
time: 35.1 us; the launch traced here: 34.9 us
  Pallas kernels  34.3 us (98%)
  between operations  0.64 us (2%)
    pallas_call x1, Pallas kernels, per_device(): pl.pallas_call(functools.partial(kernel, n_gx, n_gy), out_shape=(jax.Shap...  32.5 us
    pallas_call x1, Pallas kernels, per_device(): pl.pallas_call(put_out, out_shape=tuple((jax.ShapeDtypeStruct(o.shape, o....  1.85 us

profile of v4, /device:TPU:0, one launch (start us, length us, event | category | flops | bytes accessed | tf_op | source)
XLA Modules:
  0.0 34.9 jit_solution(13075322662093228351)
XLA Ops:
  0.6 32.5 %shard_map.111 = (f32[2,64,512]{2,1,0:T(8,128)}, f32[2,64,512]{2,1,0:T(8,128)}, bf16[2,64,512]{2,1,0:T(8,128)(2,1)}, f32[4,2048]{1,0:T(4,128)}) custom-call(f32[2,64,512]{2,1,0:T(8,128)} %shift.1, f32[2,64,512]{2,1,0:T(8,128)} %speed.1, s32[2,64,512]{2,1,0:T(8,128)} %level_h.1, s32[1,8]{1,0:T(1,128)} %bitcast.1, f32[4,2048]{1,0:T(4,128)} %warm_h.1, ...), custom_call_target="tpu_custom_call" | custom-call | tf_op jit(solution)/shard_map/pallas_call | solution.py:621
  33.1 1.9 %shard_map.112 = (f32[2,64,512]{2,1,0:T(8,128)}, f32[2,64,512]{2,1,0:T(8,128)}, bf16[2,64,512]{2,1,0:T(8,128)(2,1)}, f32[4,2048]{1,0:T(4,128)}) custom-call(f32[2,64,512]{2,1,0:T(8,128)} %get-tuple-element.8.refs_0_, f32[2,64,512]{2,1,0:T(8,128)} %get-tuple-element.9.refs_1_, bf16[2,64,512]{2,1,0:T(8,128)(2,1)} %get-tuple-element.10.refs_2_, ...), custom_call_target="tpu_custom_call" | custom-call | tf_op jit(solution)/shard_map/pallas_call | solution.py:684

commit v5 on v4

--- a/solution.py
+++ b/solution.py
@@ -523,7 +523,7 @@
     diagonal = acf[0] + offsum
     ratio = offsum / diagonal
     peak = jnp.max(ratio[8 : 8 + ch, 0:cw])
-    msend[...] = jnp.full((8, 128), peak, F32)
+    msend[...] = jnp.full((1, 128), peak, F32)
 
     def tell(k, c):
         t = lax.rem(me + k, ndev)
@@ -662,8 +662,8 @@
             vm(crows, 128),
             vm(n_gy, 4, rpd, cw),
             vm(n_gy, 4, rpd, cw),
-            vm(8, 128),
-            vm(n_gx * n_gy - 1, 8, 128),
+            vm(1, 128),
+            vm(n_gx * n_gy - 1, 1, 128),
             dma(10),
             dma(10),
             dma(4),

time: 35.1 us -> 33.2 us (0.946)
  Pallas kernels: 34.3 us -> 32.3 us
    pallas_call x1, Pallas kernels: 32.5 us -> 30.5 us  [per_device(): pl.pallas_call(functools.partial(kernel, n_gx, n_gy), out_shape=(jax.Shap...]
where the time goes in v5:
time: 33.2 us; the launch traced here: 33 us
  Pallas kernels  32.3 us (97%)
  between operations  0.64 us (2%)
    pallas_call x1, Pallas kernels, per_device(): pl.pallas_call(functools.partial(kernel, n_gx, n_gy), out_shape=(jax.Shap...  30.5 us
    pallas_call x1, Pallas kernels, per_device(): pl.pallas_call(put_out, out_shape=tuple((jax.ShapeDtypeStruct(o.shape, o....  1.85 us

profile of v5, /device:TPU:0, one launch (start us, length us, event | category | flops | bytes accessed | tf_op | source)
XLA Modules:
  0.0 33.0 jit_solution(1031362720180560012)
XLA Ops:
  0.6 30.5 %shard_map.111 = (f32[2,64,512]{2,1,0:T(8,128)}, f32[2,64,512]{2,1,0:T(8,128)}, bf16[2,64,512]{2,1,0:T(8,128)(2,1)}, f32[4,2048]{1,0:T(4,128)}) custom-call(f32[2,64,512]{2,1,0:T(8,128)} %shift.1, f32[2,64,512]{2,1,0:T(8,128)} %speed.1, s32[2,64,512]{2,1,0:T(8,128)} %level_h.1, s32[1,8]{1,0:T(1,128)} %bitcast.1, f32[4,2048]{1,0:T(4,128)} %warm_h.1, ...), custom_call_target="tpu_custom_call" | custom-call | tf_op jit(solution)/shard_map/pallas_call | solution.py:621
  31.1 1.9 %shard_map.112 = (f32[2,64,512]{2,1,0:T(8,128)}, f32[2,64,512]{2,1,0:T(8,128)}, bf16[2,64,512]{2,1,0:T(8,128)(2,1)}, f32[4,2048]{1,0:T(4,128)}) custom-call(f32[2,64,512]{2,1,0:T(8,128)} %get-tuple-element.8.refs_0_, f32[2,64,512]{2,1,0:T(8,128)} %get-tuple-element.9.refs_1_, bf16[2,64,512]{2,1,0:T(8,128)(2,1)} %get-tuple-element.10.refs_2_, ...), custom_call_target="tpu_custom_call" | custom-call | tf_op jit(solution)/shard_map/pallas_call | solution.py:684
